TPU v7x, 256 devices: a whole 4x4x8 slice. The times are simulated.
256 devices in a mesh: gx: 16 (over z, x_lo), gy: 4 (over x_hi, core), gz: 4 (over y).
Axes of the slice: x: 4 (x_hi: 2, x_lo: 2; x = x_hi * 2 + x_lo), y: 4, z: 8, core: 2. Of those that a mesh axis runs over, the one named last changes fastest.
Arguments:
- positions: float32 [3, 32, 8, 16, 128], P(None, 'gx', 'gy', 'gz'), may hold values from 0 to 1
- species: int32 [32, 8, 16, 128], P('gx', 'gy', 'gz'), may hold values from 0 to 1
- counts: int32 [32, 8, 16], P('gx', 'gy', 'gz'), may hold values from 0 to 128, as said below
Outputs:
- forces: float32 [3, 32, 8, 16, 128], P(None, 'gx', 'gy', 'gz')
- energy: float32 [32, 8, 16, 128], P('gx', 'gy', 'gz')
Inputs may be any that keep to these rules, and one draw needn't show every extreme that they name: `counts`: slots at or beyond a tile's count are empty; tiles in the lower half of the surface normal are nearly full, those above it nearly empty except for a block of tiles holding the nanoparticle.
All inputs are finite; a program needn't handle non-finite values.
Results may differ from a plain program's by a relative error of at most 0.0001.
Values sent between devices are 32-bit elements; how exact they have to be, the bound alone decides.
A program may use at most 64 MiB of HBM per device.

v0:
```python
import jax
import jax.numpy as jnp
from jax import lax
from jax.sharding import PartitionSpec as P

CUTOFF_SQUARED = 0.2025
DENSITY_BASE = 1.0
DENSITY_STEP = 0.4
EMBED_BASE = 1.0
EMBED_STEP = -0.3
PAIR_BASE = 0.6
PAIR_STEP = 0.3


def extended_2(block, sides, width, periodic):
    for axis, dim in sides:
        count = lax.axis_size(axis)
        forward = [(i, i + 1) for i in range(count - 1)]
        if periodic:
            forward.append((count - 1, 0))
        backward = [(target, source) for source, target in forward]
        low = lax.ppermute(
            lax.slice_in_dim(block, block.shape[dim] - width, None, axis=dim), axis, forward
        )
        high = lax.ppermute(lax.slice_in_dim(block, 0, width, axis=dim), axis, backward)
        block = jnp.concatenate([low, block, high], axis=dim)
    return block


def neighbour_offsets():
    return [
        (first, second, third)
        for first in (-1, 0, 1)
        for second in (-1, 0, 1)
        for third in (-1, 0, 1)
    ]


def kernels(squared):
    reach = jnp.maximum(1.0 - squared / CUTOFF_SQUARED, 0.0)
    reach_two = reach * reach
    return (
        reach_two * reach,
        reach_two * reach_two,
        -3.0 * reach_two / CUTOFF_SQUARED,
        -4.0 * reach_two * reach / CUTOFF_SQUARED,
    )


def shifted(field, offset):
    extent_x = field.shape[-4] - 2
    extent_y = field.shape[-3] - 2
    extent_z = field.shape[-2] - 2
    return field[
        ...,
        1 + offset[0] : 1 + offset[0] + extent_x,
        1 + offset[1] : 1 + offset[1] + extent_y,
        1 + offset[2] : 1 + offset[2] + extent_z,
        :,
    ]


def geometry(centre, beside, offset):
    parts = [
        beside[comp][..., None, :] + float(offset[comp]) - centre[comp][..., :, None]
        for comp in range(3)
    ]
    squared = parts[0] * parts[0] + parts[1] * parts[1] + parts[2] * parts[2]
    return (parts, squared)


def densities(extended):
    centre = shifted(extended, (0, 0, 0))
    self_mask = 1.0 - jnp.eye(centre.shape[-1], dtype=jnp.float32)
    total = jnp.zeros(centre.shape[1:], jnp.float32)
    for offset in neighbour_offsets():
        beside = shifted(extended, offset)
        parts, squared = geometry(centre, beside, offset)
        cube = kernels(squared)[0]
        weight = beside[3] * (DENSITY_BASE + DENSITY_STEP * beside[4])
        terms = cube * weight[..., None, :]
        if offset == (0, 0, 0):
            terms = terms * self_mask
        total = total + jnp.sum(terms, axis=-1)
    return total


def embedding(density, state):
    strength = state[3] * (EMBED_BASE + EMBED_STEP * state[4])
    root = jnp.sqrt(1.0 + density)
    return (-strength * root, -0.5 * strength / root)


def forces_of(extended, derivative_ext):
    centre = shifted(extended, (0, 0, 0))
    slope_own = shifted(derivative_ext, (0, 0, 0))
    dens_own = centre[3] * (DENSITY_BASE + DENSITY_STEP * centre[4])
    pair_own = centre[3] * (PAIR_BASE + PAIR_STEP * centre[4])
    self_mask = 1.0 - jnp.eye(centre.shape[-1], dtype=jnp.float32)
    total = jnp.zeros((3,) + centre.shape[1:], jnp.float32)
    pair_total = jnp.zeros(centre.shape[1:], jnp.float32)
    for offset in neighbour_offsets():
        beside = shifted(extended, offset)
        slope_beside = shifted(derivative_ext, offset)
        parts, squared = geometry(centre, beside, offset)
        cube, quart, cube_slope, quart_slope = kernels(squared)
        dens_beside = beside[3] * (DENSITY_BASE + DENSITY_STEP * beside[4])
        pair_beside = beside[3] * (PAIR_BASE + PAIR_STEP * beside[4])
        pair_weight = pair_own[..., :, None] * pair_beside[..., None, :]
        weight_pair = (
            cube_slope
            * (
                slope_own[..., :, None] * dens_beside[..., None, :]
                + slope_beside[..., None, :] * dens_own[..., :, None]
            )
            + quart_slope * pair_weight
        )
        energy_terms = quart * pair_weight
        if offset == (0, 0, 0):
            weight_pair = weight_pair * self_mask
            energy_terms = energy_terms * self_mask
        total = total + 2.0 * jnp.stack(
            [jnp.sum(weight_pair * parts[comp], axis=-1) for comp in range(3)]
        )
        pair_total = pair_total + jnp.sum(energy_terms, axis=-1)
    return (total, pair_total)


def extend(field, width):
    sideways = extended_2(field, (("gx", 1), ("gy", 2)), width, True)
    return extended_2(sideways, (("gz", 3),), width, False)


def shards(positions, species, counts):
    occupied = (lax.broadcasted_iota(jnp.int32, species.shape, 3) < counts[..., None]).astype(
        jnp.float32
    )
    state = jnp.concatenate([positions, occupied[None], species.astype(jnp.float32)[None]], axis=0)
    extended = extend(state, 1)
    density = densities(extended)
    embed, derivative = embedding(density, state)
    derivative_ext = extend(derivative[None], 1)[0]
    forces, pair_total = forces_of(extended, derivative_ext)
    return (forces, embed + 0.5 * pair_total)


def solution(mesh):
    placed = (P(None, "gx", "gy", "gz", None), P("gx", "gy", "gz", None), P("gx", "gy", "gz"))
    return jax.shard_map(
        shards,
        mesh=mesh,
        in_specs=placed,
        out_specs=(P(None, "gx", "gy", "gz", None), P("gx", "gy", "gz", None)),
        check_vma=False,
    )
```

profile of v0, /device:TPU:1, one launch (start us, length us, event | category | flops | bytes accessed | tf_op | source)
XLA Modules:
  0.0 130.3 jit_solution(1375313775262515100)
XLA Ops:
  1.5 2.1 %collective-permute-start = (f32[5,1,2,4,128]{4,3,2,1,0:T(4,128)S(1)}, f32[5,1,2,4,128]{4,3,2,1,0:T(4,128)S(1)}, u32[]{:S(2)}, u32[]{:S(2)}) collective-permute-start(f32[5,1,2,4,128]{4,3,2,1,0:T(4,128)S(1)} %get-tuple-element.368), channel_id=1, source_target_pairs={{0,16},{16,32},{32,48},{48,64},{64,80},{80,96},{96,112},{112,128},... | collective-permute-start | bytes 61448 | tf_op jit(solution)/shard_map/ppermute | solution.py:22
  3.6 5.4 %collective-permute-start.1 = (f32[5,1,2,4,128]{4,3,2,1,0:T(4,128)S(1)}, f32[5,1,2,4,128]{4,3,2,1,0:T(4,128)S(1)}, u32[]{:S(2)}, u32[]{:S(2)}) collective-permute-start(f32[5,1,2,4,128]{4,3,2,1,0:T(4,128)S(1)} %get-tuple-element.369), channel_id=1, source_target_pairs={{16,0},{32,16},{48,32},{64,48},{80,64},{96,80},{112,96},{128,112},... | collective-permute-start | bytes 61448 | tf_op jit(solution)/shard_map/ppermute | solution.py:25
  10.1 4.0 %collective-permute-start.2 = (f32[5,4,1,4,128]{4,3,2,1,0:T(4,128)S(1)}, f32[5,4,1,4,128]{4,3,2,1,0:T(4,128)S(1)}, u32[]{:S(2)}, u32[]{:S(2)}) collective-permute-start(f32[5,4,1,4,128]{4,3,2,1,0:T(4,128)S(1)} %get-tuple-element.327), channel_id=1, source_target_pairs={{0,4},{4,8},{8,12},{12,0},{1,5},{5,9},{9,13},{13,1},{2,6},{6,10},{... | collective-permute-start | bytes 122888 | tf_op jit(solution)/shard_map/ppermute | solution.py:22
  15.2 3.8 %collective-permute-done.3 = f32[5,4,1,4,128]{4,3,2,1,0:T(4,128)S(1)} collective-permute-done((f32[5,4,1,4,128]{4,3,2,1,0:T(4,128)S(1)}, f32[5,4,1,4,128]{4,3,2,1,0:T(4,128)S(1)}, u32[]{:S(2)}, u32[]{:S(2)}) %collective-permute-start.3) | collective-permute-done | bytes 40992 | tf_op jit(solution)/shard_map/ppermute | solution.py:25
  19.1 3.2 %collective-permute-start.4 = (f32[5,4,4,1,128]{4,3,2,1,0:T(1,128)S(1)}, f32[5,4,4,1,128]{4,3,2,1,0:T(1,128)S(1)}, u32[]{:S(2)}, u32[]{:S(2)}) collective-permute-start(f32[5,4,4,1,128]{4,3,2,1,0:T(1,128)S(1)} %get-tuple-element.293), channel_id=1, source_target_pairs={{0,1},{1,2},{2,3},{4,5},{5,6},{6,7},{8,9},{9,10},{10,11},{12,13},{... | collective-permute-start | bytes 122888 | tf_op jit(solution)/shard_map/ppermute | solution.py:22
  23.7 3.3 %collective-permute-done.5 = f32[5,4,4,1,128]{4,3,2,1,0:T(1,128)S(1)} collective-permute-done((f32[5,4,4,1,128]{4,3,2,1,0:T(1,128)S(1)}, f32[5,4,4,1,128]{4,3,2,1,0:T(1,128)S(1)}, u32[]{:S(2)}, u32[]{:S(2)}) %collective-permute-start.5) | collective-permute-done | bytes 40992 | tf_op jit(solution)/shard_map/ppermute | solution.py:25
  27.4 2.2 %fusion.59 = (f32[2,2,4,128]{3,2,1,0:T(4,128)S(1)}, f32[2,2,4,128]{3,2,1,0:T(4,128)S(1)}, f32[2,2,4,128]{3,2,1,0:T(4,128)S(1)}) fusion(f32[2,2,4,128]{3,2,1,0:T(4,128)S(1)} %get-tuple-element.259, f32[2,2,4,128]{3,2,1,0:T(4,128)S(1)} %get-tuple-element.261, f32[2,2,4,128]{3,2,1,0:T(4,128)S(1)} %get-tuple-element.262, ...), kind=kLoop, calls=%fused_computation.383 | loop fusion | flops 12052480 | bytes 188416 | tf_op jit(solution)/shard_map/reduce_sum | solution.py:84
  29.7 2.9 %fusion.34 = (f32[2,2,4,128]{3,2,1,0:T(4,128)S(1)}, f32[2,2,4,128]{3,2,1,0:T(4,128)S(1)}, f32[2,2,4,128]{3,2,1,0:T(4,128)S(1)}, f32[2,2,4,128]{3,2,1,0:T(4,128)S(1)}) fusion(f32[2,2,4,128]{3,2,1,0:T(4,128)S(1)} %get-tuple-element.318, f32[2,2,4,128]{3,2,1,0:T(4,128)S(1)} %get-tuple-element.320, f32[2,2,4,128]{3,2,1,0:T(4,128)S(1)} %get-tuple-element.381, ...), kind=kLoop, calls=%fused_computation.358 | loop fusion | flops 15720448 | bytes 188416 | tf_op jit(solution)/shard_map/reduce_sum | solution.py:84
  32.6 2.9 %fusion.31 = (f32[2,2,4,128]{3,2,1,0:T(4,128)S(1)}, f32[2,2,4,128]{3,2,1,0:T(4,128)S(1)}, f32[2,2,4,128]{3,2,1,0:T(4,128)S(1)}, f32[2,2,4,128]{3,2,1,0:T(4,128)S(1)}) fusion(f32[2,2,4,128]{3,2,1,0:T(4,128)S(1)} %get-tuple-element.287, f32[2,2,4,128]{3,2,1,0:T(4,128)S(1)} %get-tuple-element.373, f32[2,2,4,128]{3,2,1,0:T(4,128)S(1)} %get-tuple-element.288, ...), kind=kLoop, calls=%fused_computation.355 | loop fusion | flops 15720448 | bytes 188416 | tf_op jit(solution)/shard_map/reduce_sum | solution.py:84
  35.4 2.9 %fusion.49 = (f32[2,2,4,128]{3,2,1,0:T(4,128)S(1)}, f32[2,2,4,128]{3,2,1,0:T(4,128)S(1)}, f32[2,2,4,128]{3,2,1,0:T(4,128)S(1)}, f32[2,2,4,128]{3,2,1,0:T(4,128)S(1)}) fusion(f32[2,2,4,128]{3,2,1,0:T(4,128)S(1)} %multiply_bitcast_fusion.47, f32[2,2,4,128]{3,2,1,0:T(4,128)S(1)} %get-tuple-element.366, f32[2,2,4,128]{3,2,1,0:T(4,128)S(1)} %get-tuple-element.357, ...), kind=kLoop, calls=%fused_computation.373 | loop fusion | flops 15720448 | bytes 188416 | tf_op jit(solution)/shard_map/reduce_sum | solution.py:84
  38.3 2.9 %fusion.54 = (f32[2,2,4,128]{3,2,1,0:T(4,128)S(1)}, f32[2,2,4,128]{3,2,1,0:T(4,128)S(1)}, f32[2,2,4,128]{3,2,1,0:T(4,128)S(1)}, f32[2,2,4,128]{3,2,1,0:T(4,128)S(1)}) fusion(f32[2,2,4,128]{3,2,1,0:T(4,128)S(1)} %get-tuple-element.276, f32[2,2,4,128]{3,2,1,0:T(4,128)S(1)} %get-tuple-element.278, f32[2,2,4,128]{3,2,1,0:T(4,128)S(1)} %get-tuple-element.279, ...), kind=kLoop, calls=%fused_computation.378 | loop fusion | flops 15720448 | bytes 188416 | tf_op jit(solution)/shard_map/reduce_sum | solution.py:84
  41.2 2.9 %fusion.39 = (f32[2,2,4,128]{3,2,1,0:T(4,128)S(1)}, f32[2,2,4,128]{3,2,1,0:T(4,128)S(1)}, f32[2,2,4,128]{3,2,1,0:T(4,128)S(1)}, f32[2,2,4,128]{3,2,1,0:T(4,128)S(1)}) fusion(f32[2,2,4,128]{3,2,1,0:T(4,128)S(1)} %get-tuple-element.385, f32[2,2,4,128]{3,2,1,0:T(4,128)S(1)} %get-tuple-element.281, f32[2,2,4,128]{3,2,1,0:T(4,128)S(1)} %get-tuple-element.384, ...), kind=kLoop, calls=%fused_computation.363 | loop fusion | flops 15720448 | bytes 188416 | tf_op jit(solution)/shard_map/reduce_sum | solution.py:84
  44.1 2.9 %fusion.44 = (f32[2,2,4,128]{3,2,1,0:T(4,128)S(1)}, f32[2,2,4,128]{3,2,1,0:T(4,128)S(1)}, f32[2,2,4,128]{3,2,1,0:T(4,128)S(1)}, f32[2,2,4,128]{3,2,1,0:T(4,128)S(1)}) fusion(f32[2,2,4,128]{3,2,1,0:T(4,128)S(1)} %get-tuple-element.264, f32[2,2,4,128]{3,2,1,0:T(4,128)S(1)} %get-tuple-element.266, f32[2,2,4,128]{3,2,1,0:T(4,128)S(1)} %get-tuple-element.267, ...), kind=kLoop, calls=%fused_computation.368 | loop fusion | flops 15720448 | bytes 188416 | tf_op jit(solution)/shard_map/reduce_sum | solution.py:84
  47.2 3.6 %collective-permute-start.7 = (f32[1,1,2,4,128]{4,3,2,1,0:T(4,128)S(1)}, f32[1,1,2,4,128]{4,3,2,1,0:T(4,128)S(1)}, u32[]{:S(2)}, u32[]{:S(2)}) collective-permute-start(f32[1,1,2,4,128]{4,3,2,1,0:T(4,128)S(1)} %get-tuple-element.380), channel_id=1, source_target_pairs={{16,0},{32,16},{48,32},{64,48},{80,64},{96,80},{112,96},{128,112},... | collective-permute-start | bytes 12296 | tf_op jit(solution)/shard_map/ppermute | solution.py:25
  51.8 2.9 %collective-permute-start.8 = (f32[1,4,1,4,128]{4,3,2,1,0:T(4,128)S(1)}, f32[1,4,1,4,128]{4,3,2,1,0:T(4,128)S(1)}, u32[]{:S(2)}, u32[]{:S(2)}) collective-permute-start(f32[1,4,1,4,128]{4,3,2,1,0:T(4,128)S(1)} %get-tuple-element.375), channel_id=1, source_target_pairs={{0,4},{4,8},{8,12},{12,0},{1,5},{5,9},{9,13},{13,1},{2,6},{6,10},{... | collective-permute-start | bytes 24584 | tf_op jit(solution)/shard_map/ppermute | solution.py:22
  55.5 3.8 %collective-permute-done.9 = f32[1,4,1,4,128]{4,3,2,1,0:T(4,128)S(1)} collective-permute-done((f32[1,4,1,4,128]{4,3,2,1,0:T(4,128)S(1)}, f32[1,4,1,4,128]{4,3,2,1,0:T(4,128)S(1)}, u32[]{:S(2)}, u32[]{:S(2)}) %collective-permute-start.9) | collective-permute-done | bytes 8224 | tf_op jit(solution)/shard_map/ppermute | solution.py:25
  59.3 3.2 %collective-permute-start.10 = (f32[1,4,4,1,128]{4,3,2,1,0:T(1,128)S(1)}, f32[1,4,4,1,128]{4,3,2,1,0:T(1,128)S(1)}, u32[]{:S(2)}, u32[]{:S(2)}) collective-permute-start(f32[1,4,4,1,128]{4,3,2,1,0:T(1,128)S(1)} %get-tuple-element.370), channel_id=1, source_target_pairs={{0,1},{1,2},{2,3},{4,5},{5,6},{6,7},{8,9},{9,10},{10,11},{12,13},{... | collective-permute-start | bytes 24584 | tf_op jit(solution)/shard_map/ppermute | solution.py:22
  62.5 1.3 collective-permute-start.11
  63.8 3.1 %collective-permute-done.11 = f32[1,4,4,1,128]{4,3,2,1,0:T(1,128)S(1)} collective-permute-done((f32[1,4,4,1,128]{4,3,2,1,0:T(1,128)S(1)}, f32[1,4,4,1,128]{4,3,2,1,0:T(1,128)S(1)}, u32[]{:S(2)}, u32[]{:S(2)}) %collective-permute-start.11) | collective-permute-done | bytes 8224 | tf_op jit(solution)/shard_map/ppermute | solution.py:25
  67.0 4.6 %fusion.289 = (f32[2,2,4,128]{3,2,1,0:T(4,128)S(1)}, f32[2,2,4,128]{3,2,1,0:T(4,128)S(1)}, f32[2,2,4,128]{3,2,1,0:T(4,128)S(1)}, f32[2,2,4,128]{3,2,1,0:T(4,128)...) fusion(f32[2,2,4,128]{3,2,1,0:T(4,128)S(1)} %get-tuple-element., ...), kind=kLoop, calls=%fused_computation.613 | loop fusion | flops 16760832 | bytes 212992 | tf_op jit(solution)/shard_map/reduce_sum | solution.py:123
  71.5 4.6 %fusion.297 = (f32[2,2,4,128]{3,2,1,0:T(4,128)S(1)}, f32[2,2,4,128]{3,2,1,0:T(4,128)S(1)}, f32[2,2,4,128]{3,2,1,0:T(4,128)S(1)}, f32[2,2,4,128]{3,2,1,0:T(4,128)...) fusion(f32[2,2,4,128]{3,2,1,0:T(4,128)S(1)} %get-tuple-element., ...), kind=kLoop, calls=%fused_computation.621 | loop fusion | flops 16760832 | bytes 212992 | tf_op jit(solution)/shard_map/reduce_sum | solution.py:123
  76.1 4.6 %fusion.305 = (f32[2,2,4,128]{3,2,1,0:T(4,128)S(1)}, f32[2,2,4,128]{3,2,1,0:T(4,128)S(1)}, f32[2,2,4,128]{3,2,1,0:T(4,128)S(1)}, f32[2,2,4,128]{3,2,1,0:T(4,128)...) fusion(f32[2,2,4,128]{3,2,1,0:T(4,128)S(1)} %get-tuple-element., ...), kind=kLoop, calls=%fused_computation.629 | loop fusion | flops 16760832 | bytes 212992 | tf_op jit(solution)/shard_map/reduce_sum | solution.py:123
  80.7 4.6 %fusion.313 = (f32[2,2,4,128]{3,2,1,0:T(4,128)S(1)}, f32[2,2,4,128]{3,2,1,0:T(4,128)S(1)}, f32[2,2,4,128]{3,2,1,0:T(4,128)S(1)}, f32[2,2,4,128]{3,2,1,0:T(4,128)...) fusion(f32[2,2,4,128]{3,2,1,0:T(4,128)S(1)} %get-tuple-element., ...), kind=kLoop, calls=%fused_computation.637 | loop fusion | flops 16760832 | bytes 212992 | tf_op jit(solution)/shard_map/reduce_sum | solution.py:123
  85.3 4.6 %fusion.321 = (f32[2,2,4,128]{3,2,1,0:T(4,128)S(1)}, f32[2,2,4,128]{3,2,1,0:T(4,128)S(1)}, f32[2,2,4,128]{3,2,1,0:T(4,128)S(1)}, f32[2,2,4,128]{3,2,1,0:T(4,128)...) fusion(f32[2,2,4,128]{3,2,1,0:T(4,128)S(1)} %get-tuple-element., ...), kind=kLoop, calls=%fused_computation.645 | loop fusion | flops 16760832 | bytes 212992 | tf_op jit(solution)/shard_map/reduce_sum | solution.py:123
  89.8 4.6 %fusion.329 = (f32[2,2,4,128]{3,2,1,0:T(4,128)S(1)}, f32[2,2,4,128]{3,2,1,0:T(4,128)S(1)}, f32[2,2,4,128]{3,2,1,0:T(4,128)S(1)}, f32[2,2,4,128]{3,2,1,0:T(4,128)...) fusion(f32[2,2,4,128]{3,2,1,0:T(4,128)S(1)} %get-tuple-element., ...), kind=kLoop, calls=%fused_computation.653 | loop fusion | flops 16760832 | bytes 212992 | tf_op jit(solution)/shard_map/reduce_sum | solution.py:123
  94.4 4.6 %fusion.337 = (f32[2,2,4,128]{3,2,1,0:T(4,128)S(1)}, f32[2,2,4,128]{3,2,1,0:T(4,128)S(1)}, f32[2,2,4,128]{3,2,1,0:T(4,128)S(1)}, f32[2,2,4,128]{3,2,1,0:T(4,128)...) fusion(f32[2,2,4,128]{3,2,1,0:T(4,128)S(1)} %get-tuple-element., ...), kind=kLoop, calls=%fused_computation.661 | loop fusion | flops 16760832 | bytes 212992 | tf_op jit(solution)/shard_map/reduce_sum | solution.py:123
  99.0 4.6 %fusion.345 = (f32[2,2,4,128]{3,2,1,0:T(4,128)S(1)}, f32[2,2,4,128]{3,2,1,0:T(4,128)S(1)}, f32[2,2,4,128]{3,2,1,0:T(4,128)S(1)}, f32[2,2,4,128]{3,2,1,0:T(4,128)...) fusion(f32[2,2,4,128]{3,2,1,0:T(4,128)S(1)} %get-tuple-element., ...), kind=kLoop, calls=%fused_computation.669 | loop fusion | flops 16760832 | bytes 212992 | tf_op jit(solution)/shard_map/reduce_sum | solution.py:123
  103.5 4.6 %fusion.353 = (f32[2,2,4,128]{3,2,1,0:T(4,128)S(1)}, f32[2,2,4,128]{3,2,1,0:T(4,128)S(1)}, f32[2,2,4,128]{3,2,1,0:T(4,128)S(1)}, f32[2,2,4,128]{3,2,1,0:T(4,128)...) fusion(f32[2,2,4,128]{3,2,1,0:T(4,128)S(1)} %get-tuple-element., ...), kind=kLoop, calls=%fused_computation.677 | loop fusion | flops 16760832 | bytes 212992 | tf_op jit(solution)/shard_map/reduce_sum | solution.py:123
  108.1 4.6 %fusion.361 = (f32[2,2,4,128]{3,2,1,0:T(4,128)S(1)}, f32[2,2,4,128]{3,2,1,0:T(4,128)S(1)}, f32[2,2,4,128]{3,2,1,0:T(4,128)S(1)}, f32[2,2,4,128]{3,2,1,0:T(4,128)...) fusion(f32[2,2,4,128]{3,2,1,0:T(4,128)S(1)} %get-tuple-element., ...), kind=kLoop, calls=%fused_computation.685 | loop fusion | flops 16760832 | bytes 212992 | tf_op jit(solution)/shard_map/reduce_sum | solution.py:123
  112.7 4.6 %fusion.369 = (f32[2,2,4,128]{3,2,1,0:T(4,128)S(1)}, f32[2,2,4,128]{3,2,1,0:T(4,128)S(1)}, f32[2,2,4,128]{3,2,1,0:T(4,128)S(1)}, f32[2,2,4,128]{3,2,1,0:T(4,128)...) fusion(f32[2,2,4,128]{3,2,1,0:T(4,128)S(1)} %get-tuple-element., ...), kind=kLoop, calls=%fused_computation.693 | loop fusion | flops 16760832 | bytes 212992 | tf_op jit(solution)/shard_map/reduce_sum | solution.py:123
  117.3 7.0 %fusion.377 = (f32[2,2,4,128]{3,2,1,0:T(4,128)S(1)}, f32[2,2,4,128]{3,2,1,0:T(4,128)S(1)}, f32[2,2,4,128]{3,2,1,0:T(4,128)S(1)}, f32[2,2,4,128]{3,2,1,0:T(4,128)...) fusion(f32[2,2,4,128]{3,2,1,0:T(4,128)S(1)} %get-tuple-element., ...), kind=kLoop, calls=%fused_computation.701 | loop fusion | flops 25665536 | bytes 311296 | tf_op jit(solution)/shard_map/reduce_sum | solution.py:123
  124.2 4.6 %fusion.281 = (f32[2,2,4,128]{3,2,1,0:T(4,128)S(1)}, f32[2,2,4,128]{3,2,1,0:T(4,128)S(1)}, f32[2,2,4,128]{3,2,1,0:T(4,128)S(1)}, f32[2,2,4,128]{3,2,1,0:T(4,128)...) fusion(f32[2,2,4,128]{3,2,1,0:T(4,128)S(1)} %get-tuple-element., ...), kind=kLoop, calls=%fused_computation.605 | loop fusion | flops 16760832 | bytes 212992 | tf_op jit(solution)/shard_map/reduce_sum | solution.py:123
  (54 shorter events, 8.3 us)
Async XLA Ops:
  0.6 0.7 copy-start.2
  0.6 0.8 copy-start
  1.5 7.5 %copy-start.1 = (s32[2,2,4,128]{3,2,1,0:T(4,128)S(1)}, s32[2,2,4,128]{3,2,1,0:T(4,128)}, u32[]{:S(2)}) copy-start(s32[2,2,4,128]{3,2,1,0:T(4,128)} %param.4) | copy-start | bytes 24580
  1.5 8.6 %collective-permute-start = (f32[5,1,2,4,128]{4,3,2,1,0:T(4,128)S(1)}, f32[5,1,2,4,128]{4,3,2,1,0:T(4,128)S(1)}, u32[]{:S(2)}, u32[]{:S(2)}) collective-permute-start(f32[5,1,2,4,128]{4,3,2,1,0:T(4,128)S(1)} %get-tuple-element.368), channel_id=1, source_target_pairs={{0,16},{16,32},{32,48},{48,64},{64,80},{80,96},{96,112},{112,128},... | collective-permute-start | bytes 61448 | tf_op jit(solution)/shard_map/ppermute | solution.py:22
  3.6 6.5 %collective-permute-start.1 = (f32[5,1,2,4,128]{4,3,2,1,0:T(4,128)S(1)}, f32[5,1,2,4,128]{4,3,2,1,0:T(4,128)S(1)}, u32[]{:S(2)}, u32[]{:S(2)}) collective-permute-start(f32[5,1,2,4,128]{4,3,2,1,0:T(4,128)S(1)} %get-tuple-element.369), channel_id=1, source_target_pairs={{16,0},{32,16},{48,32},{64,48},{80,64},{96,80},{112,96},{128,112},... | collective-permute-start | bytes 61448 | tf_op jit(solution)/shard_map/ppermute | solution.py:25
  10.1 5.1 %collective-permute-start.2 = (f32[5,4,1,4,128]{4,3,2,1,0:T(4,128)S(1)}, f32[5,4,1,4,128]{4,3,2,1,0:T(4,128)S(1)}, u32[]{:S(2)}, u32[]{:S(2)}) collective-permute-start(f32[5,4,1,4,128]{4,3,2,1,0:T(4,128)S(1)} %get-tuple-element.327), channel_id=1, source_target_pairs={{0,4},{4,8},{8,12},{12,0},{1,5},{5,9},{9,13},{13,1},{2,6},{6,10},{... | collective-permute-start | bytes 122888 | tf_op jit(solution)/shard_map/ppermute | solution.py:22
  14.1 4.9 %collective-permute-start.3 = (f32[5,4,1,4,128]{4,3,2,1,0:T(4,128)S(1)}, f32[5,4,1,4,128]{4,3,2,1,0:T(4,128)S(1)}, u32[]{:S(2)}, u32[]{:S(2)}) collective-permute-start(f32[5,4,1,4,128]{4,3,2,1,0:T(4,128)S(1)} %get-tuple-element.328), channel_id=1, source_target_pairs={{4,0},{8,4},{12,8},{0,12},{5,1},{9,5},{13,9},{1,13},{6,2},{10,6},{... | collective-permute-start | bytes 122888 | tf_op jit(solution)/shard_map/ppermute | solution.py:25
  19.1 4.7 %collective-permute-start.4 = (f32[5,4,4,1,128]{4,3,2,1,0:T(1,128)S(1)}, f32[5,4,4,1,128]{4,3,2,1,0:T(1,128)S(1)}, u32[]{:S(2)}, u32[]{:S(2)}) collective-permute-start(f32[5,4,4,1,128]{4,3,2,1,0:T(1,128)S(1)} %get-tuple-element.293), channel_id=1, source_target_pairs={{0,1},{1,2},{2,3},{4,5},{5,6},{6,7},{8,9},{9,10},{10,11},{12,13},{... | collective-permute-start | bytes 122888 | tf_op jit(solution)/shard_map/ppermute | solution.py:22
  22.3 4.7 %collective-permute-start.5 = (f32[5,4,4,1,128]{4,3,2,1,0:T(1,128)S(1)}, f32[5,4,4,1,128]{4,3,2,1,0:T(1,128)S(1)}, u32[]{:S(2)}, u32[]{:S(2)}) collective-permute-start(f32[5,4,4,1,128]{4,3,2,1,0:T(1,128)S(1)} %get-tuple-element.294), channel_id=1, source_target_pairs={{1,0},{2,1},{3,2},{5,4},{6,5},{7,6},{9,8},{10,9},{11,10},{13,12},{... | collective-permute-start | bytes 122888 | tf_op jit(solution)/shard_map/ppermute | solution.py:25
  47.1 4.6 %collective-permute-start.6 = (f32[1,1,2,4,128]{4,3,2,1,0:T(4,128)S(1)}, f32[1,1,2,4,128]{4,3,2,1,0:T(4,128)S(1)}, u32[]{:S(2)}, u32[]{:S(2)}) collective-permute-start(f32[1,1,2,4,128]{4,3,2,1,0:T(4,128)S(1)} %get-tuple-element.379), channel_id=1, source_target_pairs={{0,16},{16,32},{32,48},{48,64},{64,80},{80,96},{96,112},{112,128},... | collective-permute-start | bytes 12296 | tf_op jit(solution)/shard_map/ppermute | solution.py:22
  47.2 4.6 %collective-permute-start.7 = (f32[1,1,2,4,128]{4,3,2,1,0:T(4,128)S(1)}, f32[1,1,2,4,128]{4,3,2,1,0:T(4,128)S(1)}, u32[]{:S(2)}, u32[]{:S(2)}) collective-permute-start(f32[1,1,2,4,128]{4,3,2,1,0:T(4,128)S(1)} %get-tuple-element.380), channel_id=1, source_target_pairs={{16,0},{32,16},{48,32},{64,48},{80,64},{96,80},{112,96},{128,112},... | collective-permute-start | bytes 12296 | tf_op jit(solution)/shard_map/ppermute | solution.py:25
  51.8 3.7 %collective-permute-start.8 = (f32[1,4,1,4,128]{4,3,2,1,0:T(4,128)S(1)}, f32[1,4,1,4,128]{4,3,2,1,0:T(4,128)S(1)}, u32[]{:S(2)}, u32[]{:S(2)}) collective-permute-start(f32[1,4,1,4,128]{4,3,2,1,0:T(4,128)S(1)} %get-tuple-element.375), channel_id=1, source_target_pairs={{0,4},{4,8},{8,12},{12,0},{1,5},{5,9},{9,13},{13,1},{2,6},{6,10},{... | collective-permute-start | bytes 24584 | tf_op jit(solution)/shard_map/ppermute | solution.py:22
  54.7 4.6 %collective-permute-start.9 = (f32[1,4,1,4,128]{4,3,2,1,0:T(4,128)S(1)}, f32[1,4,1,4,128]{4,3,2,1,0:T(4,128)S(1)}, u32[]{:S(2)}, u32[]{:S(2)}) collective-permute-start(f32[1,4,1,4,128]{4,3,2,1,0:T(4,128)S(1)} %get-tuple-element.376), channel_id=1, source_target_pairs={{4,0},{8,4},{12,8},{0,12},{5,1},{9,5},{13,9},{1,13},{6,2},{10,6},{... | collective-permute-start | bytes 24584 | tf_op jit(solution)/shard_map/ppermute | solution.py:25
  59.3 4.5 %collective-permute-start.10 = (f32[1,4,4,1,128]{4,3,2,1,0:T(1,128)S(1)}, f32[1,4,4,1,128]{4,3,2,1,0:T(1,128)S(1)}, u32[]{:S(2)}, u32[]{:S(2)}) collective-permute-start(f32[1,4,4,1,128]{4,3,2,1,0:T(1,128)S(1)} %get-tuple-element.370), channel_id=1, source_target_pairs={{0,1},{1,2},{2,3},{4,5},{5,6},{6,7},{8,9},{9,10},{10,11},{12,13},{... | collective-permute-start | bytes 24584 | tf_op jit(solution)/shard_map/ppermute | solution.py:22
  62.5 4.4 %collective-permute-start.11 = (f32[1,4,4,1,128]{4,3,2,1,0:T(1,128)S(1)}, f32[1,4,4,1,128]{4,3,2,1,0:T(1,128)S(1)}, u32[]{:S(2)}, u32[]{:S(2)}) collective-permute-start(f32[1,4,4,1,128]{4,3,2,1,0:T(1,128)S(1)} %get-tuple-element.371), channel_id=1, source_target_pairs={{1,0},{2,1},{3,2},{5,4},{6,5},{7,6},{9,8},{10,9},{11,10},{13,12},{... | collective-permute-start | bytes 24584 | tf_op jit(solution)/shard_map/ppermute | solution.py:25
where the time goes:
time: 131 us; the launch traced here: 130 us
  other arithmetic  84.3 us (64%)
  starting transfers between devices  27 us (21%)
  waiting for transfers between devices  17.8 us (14%)
    reduce_sum x13, other arithmetic, forces_of(): jnp.sum(weight_pair * parts[comp], axis=-1)  61.7 us
    reduce_sum x7, other arithmetic, densities(): total = total + jnp.sum(terms, axis=-1)  19.5 us
    ppermute x6, starting transfers between devices, extended_2(): lax.ppermute(lax.slice_in_dim(block, block.shape[dim] - width, None, axis...  15.5 us
    ppermute x6, waiting for transfers between devices, extended_2(): lax.ppermute(lax.slice_in_dim(block, 0, width, axis=dim), axis, backward)  14 us
    ppermute x6, starting transfers between devices, extended_2(): lax.ppermute(lax.slice_in_dim(block, 0, width, axis=dim), axis, backward)  11.5 us
    ppermute x6, waiting for transfers between devices, extended_2(): lax.ppermute(lax.slice_in_dim(block, block.shape[dim] - width, None, axis...  3.79 us
  transfers between devices with their start and end apart: 12, of which 8 were waited for; matrix products, arithmetic and copies ran while one was open for 0% of the time, Pallas kernels for 0%

commit v1 on v0

v1 whole, which is shorter than its diff:
```python
import math

import jax
import jax.numpy as jnp
from jax import lax
from jax.experimental import pallas as pl
from jax.experimental.pallas import tpu as pltpu
from jax.sharding import PartitionSpec as P

F32 = jnp.float32
BF16 = jnp.bfloat16
MESH = pl.DeviceIdType.MESH
CUTOFF_SQUARED = 0.2025
SCALE = math.sqrt(2.0 / CUTOFF_SQUARED)
TILE = 128
OWN = (2, 2, 4)
EXT = (4, 4, 6)
OFFSETS = [
    (a, b, c) for a in (-1, 0, 1) for b in (-1, 0, 1) for c in (-1, 0, 1) if (a, b, c) != (0, 0, 0)
]
ALPHA = -3.0 / CUTOFF_SQUARED
BETA = -4.0 / CUTOFF_SQUARED * 0.09
SLOPE = ALPHA / (5.0 * BETA)
HIGHEST = lax.Precision.HIGHEST
NT = (((1,), (1,)), ((), ()))


def pieces(v):
    first = v.astype(BF16).astype(F32)
    rest = v - first
    second = rest.astype(BF16).astype(F32)
    return first, second, rest - second


def beside_features(v):
    a, b, c = pieces(v)
    return jnp.concatenate([a, b, a, b, c, a], axis=0).astype(BF16)


def own_features(v):
    a, b, c = pieces(v)
    return jnp.concatenate([a, a, b, b, a, c], axis=0).T.astype(BF16)


def rows_of(*rows):
    row = lax.broadcasted_iota(jnp.int32, (8, TILE), 0)
    out = jnp.zeros((8, TILE), F32)
    for index, value in enumerate(rows):
        if value is not None:
            out = jnp.where(row == index, value, out)
    return out


def tile_of(index, extent):
    plane = extent[1] * extent[2]
    return index // plane, (index // extent[2]) % extent[1], index % extent[2]


def span(offset, own, sending):
    if offset == 0:
        return pl.ds(1, own)
    if sending:
        return pl.ds(own if offset > 0 else 1, 1)
    return pl.ds(0 if offset > 0 else own + 1, 1)


def region(offset, sending):
    return tuple(span(o, n, sending) for o, n in zip(offset, OWN))


def exchange_kernel(
    sizes, pos_ref, spec_ref, count_ref, full_ref, embed_ref, wire, slope, beside, sends, recvs
):
    me = [lax.axis_index(name) for name in ("gx", "gy", "gz")]

    def peer(offset):
        return tuple(lax.rem(m + o + n, n) for m, o, n in zip(me, offset, sizes))

    barrier = pltpu.get_barrier_semaphore()
    for offset in OFFSETS:
        pl.semaphore_signal(barrier, inc=1, device_id=peer(offset), device_id_type=MESH)

    lane = lax.broadcasted_iota(jnp.int32, (1, TILE), 1)
    row4 = lax.broadcasted_iota(jnp.int32, (4, TILE), 0)
    for x in range(OWN[0]):
        for y in range(OWN[1]):
            for z in range(OWN[2]):
                kind = spec_ref[x, y, z : z + 1, :]
                weight = jnp.where(
                    lane < count_ref[x, y, z], jnp.where(kind == 1, 7.0, 5.0), 0.0
                )
                value = jnp.broadcast_to(weight, (4, TILE))
                for comp in range(3):
                    value = jnp.where(row4 == comp, pos_ref[comp, x, y, z : z + 1, :], value)
                wire[x + 1, y + 1, z + 1] = value
    pl.semaphore_wait(barrier, len(OFFSETS))

    def copies(ref, which):
        return [
            pltpu.make_async_remote_copy(
                src_ref=ref.at[region(offset, True)],
                dst_ref=ref.at[region(offset, False)],
                send_sem=sends.at[which, k],
                recv_sem=recvs.at[which, k],
                device_id=peer(offset),
                device_id_type=MESH,
            )
            for k, offset in enumerate(OFFSETS)
        ]

    state_copies = copies(wire, 0)
    for copy in state_copies:
        copy.start()
    for copy in state_copies:
        copy.wait()

    below = me[2] > 0
    above = me[2] < sizes[2] - 1

    def weights(z, value):
        inside = jnp.where(
            z == 0, below.astype(F32), jnp.where(z == EXT[2] - 1, above.astype(F32), 1.0)
        )
        return value[3:4] * inside

    def place(x, y, z, value):
        cx = (value[0:1] + (x - 2).astype(F32)) * SCALE
        cy = (value[1:2] + (y - 2).astype(F32)) * SCALE
        cz = (value[2:3] + (z - 3).astype(F32)) * SCALE
        return cx, cy, cz, 0.5 * (cx * cx + cy * cy + cz * cz)

    def prepare(index, _):
        x, y, z = tile_of(index, EXT)
        value = wire[x, y, z]
        cx, cy, cz, norm = place(x, y, z, value)
        weight = weights(z, value)
        root = jnp.where(weight > 6.0, 1.4 ** (1.0 / 3.0), jnp.where(weight > 0.0, 1.0, 0.0))
        pair = jnp.where(weight > 0.0, 0.5 * weight - 0.5, 0.0)
        beside[x * EXT[1] + y, :, pl.ds(pl.multiple_of(z * TILE, TILE), TILE)] = beside_features(
            rows_of(root * cx, root * cy, root * cz, root, -root * norm)
        )
        full_ref[x, y, z] = rows_of(cx, cy, cz, weight, 1.0, -norm, None, pair)
        return _

    lax.fori_loop(0, EXT[0] * EXT[1] * EXT[2], prepare, 0)

    ones = jnp.ones((8, TILE), F32)
    half = 32

    def density(index, _):
        x, y, z = tile_of(index, OWN)
        value = wire[x + 1, y + 1, z + 1]
        cx, cy, cz, norm = place(x + 1, y + 1, z + 1, value)
        own = own_features(rows_of(cx, cy, cz, 1.0 - norm, 1.0))
        totals = []
        for part in range(TILE // half):
            rows = own[part * half : (part + 1) * half]
            total = jnp.zeros((half, TILE), F32)
            for dx in range(3):
                for dy in range(3):
                    there = beside[
                        (x + dx) * EXT[1] + y + dy,
                        :,
                        pl.ds(pl.multiple_of(z * TILE, TILE), 3 * TILE),
                    ]
                    reach = jnp.dot(rows, there, preferred_element_type=F32)
                    reach = jnp.maximum(reach, 0.0)
                    cube = reach * reach * reach
                    middle = cube[:, TILE : 2 * TILE]
                    if (dx, dy) == (1, 1):
                        here = lax.broadcasted_iota(jnp.int32, (half, TILE), 0) + part * half
                        self_pair = here == lax.broadcasted_iota(jnp.int32, (half, TILE), 1)
                        middle = jnp.where(self_pair, 0.0, middle)
                    total = total + cube[:, :TILE] + middle + cube[:, 2 * TILE :]
            totals.append(total)
        total = jnp.concatenate(totals, axis=0)
        result = lax.dot_general(ones, total, NT, precision=HIGHEST, preferred_element_type=F32)
        root = jnp.sqrt(1.0 + result[0:1])
        weight = value[3:4]
        strength = jnp.where(weight > 6.0, 0.7, jnp.where(weight > 0.0, 1.0, 0.0))
        embed_ref[x, y, z] = -strength * root
        slope[x + 1, y + 1, z + 1] = -0.5 * SLOPE * strength / root
        return _

    lax.fori_loop(0, OWN[0] * OWN[1] * OWN[2], density, 0)

    slope_copies = copies(slope, 1)
    for copy in slope_copies:
        copy.start()
    for copy in slope_copies:
        copy.wait()

    def finish(index, _):
        x, y, z = tile_of(index, EXT)
        full_ref[x, y, z, 6:7, :] = jnp.where(
            full_ref[x, y, z, 3:4, :] > 0.0, slope[x, y, z], 0.0
        )
        return _

    lax.fori_loop(0, EXT[0] * EXT[1] * EXT[2], finish, 0)


def force_kernel(full_ref, embed_ref, forces_ref, energy_ref, beside, sums):
    row = lax.broadcasted_iota(jnp.int32, (8, TILE), 0)
    masks = ((row < 3) | (row == 4) | (row == 5), (row == 3) | (row == 6), row == 7)

    def prepare(index, _):
        x, y, z = tile_of(index, EXT)
        value = full_ref[x, y, z]
        for k, mask in enumerate(masks):
            beside[k, x * EXT[1] + y, :, pl.ds(pl.multiple_of(z * TILE, TILE), TILE)] = (
                beside_features(jnp.where(mask, value, 0.0))
            )
        return _

    lax.fori_loop(0, EXT[0] * EXT[1] * EXT[2], prepare, 0)
    half = 32

    def forces(index, _):
        x, y, z = tile_of(index, OWN)
        value = full_ref[x + 1, y + 1, z + 1]
        own_value = jnp.where(row == 3, value[6:7], value)
        own_value = jnp.where(row == 4, 1.0 + value[5:6], own_value)
        own_value = jnp.where(row == 5, 1.0, own_value)
        own_value = jnp.where(row == 6, value[3:4], own_value)
        own = own_features(own_value)
        lanes = lax.broadcasted_iota(jnp.int32, (half, TILE), 1)
        for part in range(TILE // half):
            rows = own[part * half : (part + 1) * half]
            total = [jnp.zeros((half, TILE), F32) for _ in range(5)]
            for dx in range(3):
                for dy in range(3):
                    at = (
                        (x + dx) * EXT[1] + y + dy,
                        slice(None),
                        pl.ds(pl.multiple_of(z * TILE, TILE), 3 * TILE),
                    )
                    reach, both, pair = (
                        jnp.dot(rows, beside[(k,) + at], preferred_element_type=F32)
                        for k in range(3)
                    )
                    for dz in range(3):
                        cut = slice(dz * TILE, (dz + 1) * TILE)
                        q = jnp.maximum(reach[:, cut], 0.0)
                        if (dx, dy, dz) == (1, 1, 1):
                            here = lax.broadcasted_iota(jnp.int32, (half, TILE), 0) + part * half
                            q = jnp.where(here == lanes, 0.0, q)
                        square = q * q
                        pull = square * (q * pair[:, cut])
                        coef = pull + square * both[:, cut]
                        there = full_ref[x + dx, y + dy, z + dz]
                        for comp in range(3):
                            total[comp] = total[comp] + coef * there[comp : comp + 1]
                        total[3] = total[3] + coef
                        total[4] = total[4] + pull * q
            column = jnp.zeros((half, TILE), F32)
            for k in range(5):
                column = jnp.where(lanes == k, jnp.sum(total[k], axis=1, keepdims=True), column)
            sums[part * half : (part + 1) * half, :] = column
        result = sums[...].T[:8]
        coef = result[3:4]
        moved = (2.0 * BETA / SCALE) * (result - value * coef)
        energy = embed_ref[x, y, z] + (0.5 * 0.09) * result[4:5]
        energy_ref[index] = jnp.where(row == 3, energy, moved)
        return _

    lax.fori_loop(0, OWN[0] * OWN[1] * OWN[2], forces, 0)


def shards(sizes, positions, species, counts):
    vmem = pl.BlockSpec(memory_space=pltpu.VMEM)
    full, embed = pl.pallas_call(
        lambda *refs: exchange_kernel(sizes, *refs),
        name="exchange",
        out_shape=(
            jax.ShapeDtypeStruct(EXT + (8, TILE), F32),
            jax.ShapeDtypeStruct(OWN + (1, TILE), F32),
        ),
        in_specs=[vmem, vmem, pl.BlockSpec(memory_space=pltpu.SMEM)],
        out_specs=(vmem, vmem),
        scratch_shapes=[
            pltpu.VMEM(EXT + (4, TILE), F32),
            pltpu.VMEM(EXT + (1, TILE), F32),
            pltpu.VMEM((EXT[0] * EXT[1], 48, EXT[2] * TILE), BF16),
            pltpu.SemaphoreType.DMA((2, len(OFFSETS))),
            pltpu.SemaphoreType.DMA((2, len(OFFSETS))),
        ],
        compiler_params=pltpu.CompilerParams(collective_id=0, has_side_effects=True),
    )(positions, species, counts)
    result = pl.pallas_call(
        lambda full_ref, embed_ref, out_ref, *scratch: force_kernel(
            full_ref, embed_ref, None, out_ref, *scratch
        ),
        name="forces",
        out_shape=jax.ShapeDtypeStruct((OWN[0] * OWN[1] * OWN[2], 8, TILE), F32),
        in_specs=[vmem, vmem],
        out_specs=vmem,
        scratch_shapes=[
            pltpu.VMEM((3, EXT[0] * EXT[1], 48, EXT[2] * TILE), BF16),
            pltpu.VMEM((TILE, TILE), F32),
        ],
    )(full, embed)
    result = result.reshape(OWN + (8, TILE))
    return jnp.moveaxis(result[..., :3, :], 3, 0), result[..., 3, :]


def solution(mesh):
    placed = (P(None, "gx", "gy", "gz", None), P("gx", "gy", "gz", None), P("gx", "gy", "gz"))
    sizes = tuple(mesh.shape[name] for name in ("gx", "gy", "gz"))
    return jax.shard_map(
        lambda *args: shards(sizes, *args),
        mesh=mesh,
        in_specs=placed,
        out_specs=(P(None, "gx", "gy", "gz", None), P("gx", "gy", "gz", None)),
        check_vma=False,
    )
```

time: 131 us -> 73.2 us (0.56)
  other arithmetic: 84.3 us -> 0 us
  Pallas kernels: 0 us -> 69.4 us
  starting transfers between devices: 27 us -> 0 us
  waiting for transfers between devices: 17.8 us -> 0 us
  local copies, waits for them, and re-layouts: 0.09 us -> 2.9 us
    reduce_sum x20 -> x0, other arithmetic: 81.2 us -> none  [the longest x13 61.7 us: forces_of(): jnp.sum(weight_pair * parts[comp], axis=-1)]
    pallas_call x0 -> x2, Pallas kernels: none -> 69.4 us  [the longest x1 41.9 us: shards(): pl.pallas_call(lambda *refs: exchange_kernel(sizes, *refs), name='exchang...]
    ppermute x12 -> x0, starting transfers between devices: 27 us -> none  [the longest x6 15.5 us: extended_2(): lax.ppermute(lax.slice_in_dim(block, block.shape[dim] - width, None, axis...]
    ppermute x12 -> x0, waiting for transfers between devices: 17.8 us -> none  [the longest x6 14 us: extended_2(): lax.ppermute(lax.slice_in_dim(block, 0, width, axis=dim), axis, backward)]
    slice x6 -> x2, local copies, waits for them, and re-layouts: 0.07 us -> 2.29 us  [shards(): return (jnp.moveaxis(result[..., :3, :], 3, 0), result[..., 3, :])]
    add x6 -> x0, other arithmetic: 1.53 us -> none  [the longest x1 0.75 us: forces_of(): total + 2.0 * jnp.stack([jnp.sum(weight_pair * parts[comp], axis=-1) for...]
  transfers between devices with their start and end apart: 12 -> 0, of which waited for: 8 -> 0; matrix products, arithmetic and copies ran while one was open for 0% -> 0% of each run, Pallas kernels for 0% -> 0%
where the time goes in v1:
time: 73.2 us; the launch traced here: 72.9 us
  Pallas kernels  69.4 us (95%)
  local copies, waits for them, and re-layouts  2.9 us (4%)
    pallas_call x1, Pallas kernels, shards(): pl.pallas_call(lambda *refs: exchange_kernel(sizes, *refs), name='exchang...  41.9 us
    pallas_call x1, Pallas kernels, shards(): pl.pallas_call(lambda full_ref, embed_ref, out_ref, *scratch: force_kerne...  27.5 us
    slice x2, local copies, waits for them, and re-layouts, shards(): return (jnp.moveaxis(result[..., :3, :], 3, 0), result[..., 3, :])  2.29 us

profile of v1, /device:TPU:1, one launch (start us, length us, event | category | flops | bytes accessed | tf_op | source)
XLA Modules:
  0.0 72.9 jit_solution(12060856349271770700)
XLA Ops:
  0.6 41.9 %exchange.1 = (f32[4,4,6,8,128]{4,3,2,1,0:T(8,128)}, f32[2,2,4,1,128]{4,3,2,1,0:T(1,128)}) custom-call(f32[3,2,2,4,128]{4,3,2,1,0:T(4,128)} %refs_0_.1, s32[2,2,4,128]{3,2,1,0:T(4,128)} %refs_1_.1, s32[2,2,4]{2,1,0:T(2,128)} %refs_2_.1), custom_call_target="tpu_custom_call" | custom-call | tf_op jit(solution)/shard_map/exchange/pallas_call | solution.py:272
  42.5 27.5 %forces.1 = f32[16,8,128]{2,1,0:T(8,128)} custom-call(f32[4,4,6,8,128]{4,3,2,1,0:T(8,128)} %get-tuple-element.4.full_ref, f32[2,2,4,1,128]{4,3,2,1,0:T(1,128)} %get-tuple-element.5.embed_ref), custom_call_target="tpu_custom_call" | custom-call | tf_op jit(solution)/shard_map/forces/pallas_call | solution.py:290
  70.0 1.4 %slice.9 = f32[2,2,4,1,128]{4,3,2,1,0:T(1,128)} slice(f32[2,2,4,8,128]{4,3,2,1,0:T(8,128)} %bitcast.7), slice={[0:2], [0:2], [0:4], [3:4], [0:128]} | slice | bytes 16384 | tf_op jit(solution)/shard_map/slice | solution.py:304
  71.5 0.8 %slice.8 = f32[2,2,4,3,128]{4,3,2,1,0:T(4,128)S(1)} slice(f32[2,2,4,8,128]{4,3,2,1,0:T(8,128)} %bitcast.8), slice={[0:2], [0:2], [0:4], [0:3], [0:128]} | slice | bytes 49152 | tf_op jit(solution)/shard_map/slice | solution.py:304
  72.3 0.6 copy.10

commit v2 on v1

v2 whole, which is shorter than its diff:
```python
import math

import jax
import jax.numpy as jnp
from jax import lax
from jax.experimental import pallas as pl
from jax.experimental.pallas import tpu as pltpu
from jax.sharding import PartitionSpec as P

F32 = jnp.float32
BF16 = jnp.bfloat16
MESH = pl.DeviceIdType.MESH
CUTOFF_SQUARED = 0.2025
SCALE = math.sqrt(2.0 / CUTOFF_SQUARED)
TILE = 128
OWN = (2, 2, 4)
EXT = (4, 4, 6)
OFFSETS = [
    (a, b, c) for a in (-1, 0, 1) for b in (-1, 0, 1) for c in (-1, 0, 1) if (a, b, c) != (0, 0, 0)
]
ALPHA = -3.0 / CUTOFF_SQUARED
BETA = -4.0 / CUTOFF_SQUARED * 0.09
SLOPE = ALPHA / (5.0 * BETA)
PART = 128
FORCE_PART = 64
GROUP = 6
HIGHEST = lax.Precision.HIGHEST
NT = (((1,), (1,)), ((), ()))


def pieces(v):
    first = v.astype(BF16).astype(F32)
    rest = v - first
    second = rest.astype(BF16).astype(F32)
    return first, second, rest - second


def beside_features(v):
    a, b, c = pieces(v)
    return jnp.concatenate([a, b, a, b, c, a], axis=0).astype(BF16)


def own_features(v):
    a, b, c = pieces(v)
    return jnp.concatenate([a, a, b, b, a, c], axis=0).T.astype(BF16)


def rows_of(*rows):
    row = lax.broadcasted_iota(jnp.int32, (8, TILE), 0)
    out = jnp.zeros((8, TILE), F32)
    for index, value in enumerate(rows):
        if value is not None:
            out = jnp.where(row == index, value, out)
    return out


def tile_of(index, extent):
    plane = extent[1] * extent[2]
    return index // plane, (index // extent[2]) % extent[1], index % extent[2]


def span(offset, own, sending):
    if offset == 0:
        return pl.ds(1, own)
    if sending:
        return pl.ds(own if offset > 0 else 1, 1)
    return pl.ds(0 if offset > 0 else own + 1, 1)


def region(offset, sending):
    return tuple(span(o, n, sending) for o, n in zip(offset, OWN))


def exchange_kernel(
    sizes,
    pos_ref,
    spec_ref,
    count_ref,
    full_ref,
    embed_ref,
    near_ref,
    held_ref,
    wire,
    slope,
    beside,
    own,
    totals,
    reach_rows,
    sends,
    recvs,
):
    me = [lax.axis_index(name) for name in ("gx", "gy", "gz")]

    def peer(offset):
        return tuple(lax.rem(m + o + n, n) for m, o, n in zip(me, offset, sizes))

    barrier = pltpu.get_barrier_semaphore()
    for offset in OFFSETS:
        pl.semaphore_signal(barrier, inc=1, device_id=peer(offset), device_id_type=MESH)

    lane = lax.broadcasted_iota(jnp.int32, (1, TILE), 1)
    row4 = lax.broadcasted_iota(jnp.int32, (4, TILE), 0)
    for x in range(OWN[0]):
        for y in range(OWN[1]):
            for z in range(OWN[2]):
                kind = spec_ref[x, y, z : z + 1, :]
                weight = jnp.where(
                    lane < count_ref[x, y, z], jnp.where(kind == 1, 7.0, 5.0), 0.0
                )
                value = jnp.broadcast_to(weight, (4, TILE))
                for comp in range(3):
                    value = jnp.where(row4 == comp, pos_ref[comp, x, y, z : z + 1, :], value)
                wire[x + 1, y + 1, z + 1] = value
    pl.semaphore_wait(barrier, len(OFFSETS))

    def copies(ref, which):
        return [
            pltpu.make_async_remote_copy(
                src_ref=ref.at[region(offset, True)],
                dst_ref=ref.at[region(offset, False)],
                send_sem=sends.at[which, k],
                recv_sem=recvs.at[which, k],
                device_id=peer(offset),
                device_id_type=MESH,
            )
            for k, offset in enumerate(OFFSETS)
        ]

    state_copies = copies(wire, 0)
    for copy in state_copies:
        copy.start()

    low = (me[2] > 0).astype(F32)
    high = (me[2] < sizes[2] - 1).astype(F32)

    def prepare(x, y, z):
        value = wire[x, y, z]
        weight = value[3:4] * (low if z == 0 else high if z == EXT[2] - 1 else 1.0)
        cx = (value[0:1] + (x - 2).astype(F32)) * SCALE
        cy = (value[1:2] + (y - 2).astype(F32)) * SCALE
        cz = (value[2:3] + float(z - 3)) * SCALE
        norm = 0.5 * (cx * cx + cy * cy + cz * cz)
        root = jnp.where(weight > 6.0, 1.4 ** (1.0 / 3.0), jnp.where(weight > 0.0, 1.0, 0.0))
        pair = jnp.where(weight > 0.0, 0.5 * weight - 0.5, 0.0)
        full = rows_of(cx, cy, cz, weight, 1.0, -norm, None, pair)
        full_ref[x, y, z] = full
        row = lax.broadcasted_iota(jnp.int32, (8, TILE), 0)
        part = root * jnp.where(row == 3, 1.0, jnp.where(row == 4, -norm, full))
        beside[x * EXT[1] + y, :, z * TILE : (z + 1) * TILE] = beside_features(
            jnp.where(row < 5, part, 0.0)
        )
        return full

    def prepare_own(index, _):
        x, y = 1 + index // OWN[1], 1 + index % OWN[1]
        for z in (0, EXT[2] - 1):
            beside[x * EXT[1] + y, :, z * TILE : (z + 1) * TILE] = jnp.zeros((48, TILE), BF16)
        for z in range(OWN[2]):
            full = prepare(x, y, z + 1)
            row = lax.broadcasted_iota(jnp.int32, (8, TILE), 0)
            value = jnp.where(row == 3, 1.0 + full[5:6], jnp.where(row < 5, full, 0.0))
            own[index * OWN[2] + z] = own_features(value)
        return _

    lax.fori_loop(0, OWN[0] * OWN[1], prepare_own, 0)

    def cubes(rows, there):
        value = jnp.maximum(jnp.dot(rows, there, preferred_element_type=F32), 0.0)
        return value * value * value

    def blocks(value):
        return sum(
            value[:, k * TILE : (k + 1) * TILE] for k in range(1, value.shape[1] // TILE)
        ) + value[:, :TILE]

    def window(column, z, width=3):
        return beside[column, :, pl.ds(pl.multiple_of(z * TILE, TILE), width * TILE)]

    parts = TILE // PART

    def inner(index, _):
        x, y, z = tile_of(index, OWN)
        for part in range(parts):
            cut = slice(part * PART, (part + 1) * PART)
            rows = own[index, cut]
            total = jnp.zeros((PART, TILE), F32)
            for dx in range(OWN[0]):
                for dy in range(OWN[1]):
                    there = lax.rem(x + dx, OWN[0]) + 1, lax.rem(y + dy, OWN[1]) + 1
                    cube = cubes(rows, window(there[0] * EXT[1] + there[1], z))
                    if (dx, dy) == (0, 0):
                        here = lax.broadcasted_iota(jnp.int32, (PART, TILE), 0) + part * PART
                        self_pair = here == lax.broadcasted_iota(jnp.int32, (PART, TILE), 1)
                        middle = jnp.where(self_pair, 0.0, cube[:, TILE : 2 * TILE])
                        total = total + cube[:, :TILE] + middle + cube[:, 2 * TILE :]
                    else:
                        total = total + blocks(cube)
            totals[index, cut] = total
        return _

    lax.fori_loop(0, OWN[0] * OWN[1] * OWN[2], inner, 0)

    for copy in state_copies:
        copy.wait()

    def prepare_side(index, _):
        x = jnp.where(index < 4, 0, jnp.where(index < 8, EXT[0] - 1, 1 + (index - 8) // 2))
        y = jnp.where(index < 8, lax.rem(index, 4), (EXT[1] - 1) * lax.rem(index, 2))
        for z in range(EXT[2]):
            prepare(x, y, z)
        return _

    lax.fori_loop(0, EXT[0] * EXT[1] - OWN[0] * OWN[1], prepare_side, 0)

    def prepare_ends(index, _):
        for z in (0, EXT[2] - 1):
            prepare(1 + index // OWN[1], 1 + index % OWN[1], z)
        return _

    lax.fori_loop(0, OWN[0] * OWN[1], prepare_ends, 0)

    ones = jnp.ones((8, TILE), F32)

    def ends(index, _):
        column, upper = index // 2, lax.rem(index, 2)
        tile = column * OWN[2] + upper * (OWN[2] - 1)
        for part in range(parts):
            cut = slice(part * PART, (part + 1) * PART)
            rows = own[tile, cut]
            total = totals[tile, cut]
            for x in range(OWN[0]):
                for y in range(OWN[1]):
                    there = (x + 1) * EXT[1] + y + 1
                    total = total + cubes(rows, window(there, upper * (EXT[2] - 1), 1))
            totals[tile, cut] = total
        return _

    lax.fori_loop(0, 2 * OWN[0] * OWN[1], ends, 0)

    def outer(index, _):
        x, y, z = tile_of(index, OWN)
        side_x, side_y = x * (EXT[0] - 1), y * (EXT[1] - 1)
        columns = [side_x * EXT[1] + y + dy for dy in range(3)]
        columns += [(dx + 1) * EXT[1] + side_y for dx in range(OWN[0])]
        for part in range(parts):
            cut = slice(part * PART, (part + 1) * PART)
            rows = own[index, cut]
            total = totals[index, cut]
            for column in columns:
                total = total + blocks(cubes(rows, window(column, z)))
            totals[index, cut] = total
        result = lax.dot_general(
            ones, totals[index], NT, precision=HIGHEST, preferred_element_type=F32
        )
        root = jnp.sqrt(1.0 + result[0:1])
        weight = wire[x + 1, y + 1, z + 1, 3:4, :]
        strength = jnp.where(weight > 6.0, 0.7, jnp.where(weight > 0.0, 1.0, 0.0))
        embed_ref[index] = -strength * root
        slope[x + 1, y + 1, z + 1] = -0.5 * SLOPE * strength / root
        return _

    lax.fori_loop(0, OWN[0] * OWN[1] * OWN[2], outer, 0)

    slope_copies = copies(slope, 1)
    for copy in slope_copies:
        copy.start()

    def distances(index, _):
        x, y, z = tile_of(index, OWN)
        for k, offset in enumerate(OFFSETS):
            at = tuple(a + 1 + o for a, o in zip((x, y, z), offset))
            there = wire[at]
            far = None
            for comp, o in enumerate(offset):
                if o:
                    gap = there[comp : comp + 1] if o > 0 else 1.0 - there[comp : comp + 1]
                    far = gap * gap if far is None else far + gap * gap
            weight = full_ref[at + (slice(3, 4),)]
            reach_rows[index, k : k + 1, :] = jnp.where(weight > 0.0, far, 9.0)
        for k in range(len(OFFSETS), 32):
            reach_rows[index, k : k + 1, :] = jnp.full((1, TILE), 9.0, F32)
        return _

    lax.fori_loop(0, OWN[0] * OWN[1] * OWN[2], distances, 0)

    first = lax.broadcasted_iota(jnp.int32, (TILE, TILE), 0)
    second = lax.broadcasted_iota(jnp.int32, (TILE, TILE), 1)
    earlier = (first < second).astype(F32).astype(BF16)

    def compress(group, _):
        rows = reach_rows[pl.ds(group * 4, 4)].reshape(TILE, TILE)
        near = rows < CUTOFF_SQUARED * 1.00002
        flags = near.astype(F32).astype(BF16)
        before = jnp.dot(flags, earlier, preferred_element_type=F32).astype(jnp.int32)
        word = jnp.where(near, 16384 + second * 128 + (second - before), 0)
        for bit in range(7):
            moved = pltpu.roll(word, TILE - (1 << bit), 1)
            stay = jnp.where((word & (1 << bit)) != 0, 0, word)
            word = jnp.where((moved & (1 << bit)) != 0, moved, stay)
        near_ref[pl.ds(group * 4, 4)] = ((word >> 7) & 127).reshape(4, 32, TILE)
        held = lax.dot_general(
            jnp.ones((8, TILE), BF16), flags, NT, preferred_element_type=F32
        )
        held_ref[:, pl.ds(pl.multiple_of(group * TILE, TILE), TILE)] = held[0:1].astype(jnp.int32)
        return _

    lax.fori_loop(0, 4, compress, 0)

    for copy in slope_copies:
        copy.wait()

    def finish(index, _):
        for z in range(EXT[2]):
            at = (index // EXT[1], lax.rem(index, EXT[1]), z)
            value = slope[at]
            if z in (0, EXT[2] - 1):
                value = value * (high if z else low)
            full_ref[at + (slice(6, 7),)] = value
        return _

    lax.fori_loop(0, EXT[0] * EXT[1], finish, 0)


def force_kernel(
    full_ref, embed_ref, near_ref, held_ref, forces_ref, energy_ref, packed, sums, results, total_ref
):
    row = lax.broadcasted_iota(jnp.int32, (8, TILE), 0)
    lane = lax.broadcasted_iota(jnp.int32, (8, TILE), 1)
    masks = ((row < 3) | (row == 4) | (row == 5), (row == 3) | (row == 6), row == 7)
    tiles = OWN[0] * OWN[1] * OWN[2]

    def pack(index, _):
        x, y, z = tile_of(index, OWN)
        packed[index, 0] = full_ref[x + 1, y + 1, z + 1]
        filled = 0
        current = jnp.zeros((8, TILE), F32)
        for k, offset in enumerate(OFFSETS):
            held = held_ref[0, index * 32 + k]
            there = full_ref[tuple(a + 1 + o for a, o in zip((x, y, z), offset))]
            places = jnp.broadcast_to(near_ref[index, k : k + 1, :], (8, TILE))
            value = jnp.take_along_axis(there, places, axis=1, mode="promise_in_bounds")
            value = jnp.where(lane < held, value, 0.0)
            start = filled & (TILE - 1)
            value = pltpu.roll(value, start, 1)
            behind = lane >= start
            merged = jnp.where(behind, value, current)
            beyond = jnp.where(behind, 0.0, value)
            chunk = 1 + (filled >> 7)
            packed[index, chunk] = merged
            packed[index, chunk + 1] = beyond
            filled = filled + held
            current = jnp.where((filled >> 7) + 1 > chunk, beyond, merged)
        for k in range(GROUP):
            packed[index, 2 + (filled >> 7) + k] = jnp.zeros((8, TILE), F32)
        total_ref[index] = filled
        return _

    lax.fori_loop(0, tiles, pack, 0)

    def group(index, own, start, count, with_self):
        lanes = lax.broadcasted_iota(jnp.int32, (FORCE_PART, TILE), 1)
        values = [packed[index, start + k] for k in range(count)]
        features = [
            [beside_features(jnp.where(mask, value, 0.0)) for mask in masks] for value in values
        ]
        for part in range(TILE // FORCE_PART):
            rows = own[part * FORCE_PART : (part + 1) * FORCE_PART]
            total = [jnp.zeros((FORCE_PART, TILE), F32) for _ in range(5)]
            for k, value in enumerate(values):
                reach, both, pair = (
                    jnp.dot(rows, feature, preferred_element_type=F32) for feature in features[k]
                )
                q = jnp.maximum(reach, 0.0)
                if with_self and k == 0:
                    here = lax.broadcasted_iota(jnp.int32, (FORCE_PART, TILE), 0) + part * FORCE_PART
                    q = jnp.where(here == lanes, 0.0, q)
                square = q * q
                pull = square * (q * pair)
                coef = pull + square * both
                for comp in range(3):
                    total[comp] = total[comp] + coef * value[comp : comp + 1]
                total[3] = total[3] + coef
                total[4] = total[4] + pull * q
            column = jnp.zeros((FORCE_PART, TILE), F32)
            for k in range(5):
                column = jnp.where(lanes == k, jnp.sum(total[k], axis=1, keepdims=True), column)
            sums[part * FORCE_PART : (part + 1) * FORCE_PART, :] = column
        return sums[...].T[:8]

    def own_rows(value):
        out = jnp.where(row == 3, value[6:7], value)
        out = jnp.where(row == 4, 1.0 + value[5:6], out)
        out = jnp.where(row == 5, 1.0, out)
        return own_features(jnp.where(row == 6, value[3:4], out))

    def forces(index, _):
        value = packed[index, 0]
        own = own_rows(value)
        chunks = 1 + ((total_ref[index] + TILE - 1) >> 7)
        result = group(index, own, 0, GROUP, True)
        more = (chunks - GROUP + 1) // 2
        result = lax.fori_loop(
            0,
            jnp.maximum(more, 0),
            lambda step, carry: carry + group(index, own, GROUP + 2 * step, 2, False),
            result,
        )
        moved = (2.0 * BETA / SCALE) * (result - value * result[3:4])
        energy = embed_ref[index] + (0.5 * 0.09) * result[4:5]
        results[index] = jnp.where(row == 3, energy, moved)
        return _

    lax.fori_loop(0, tiles, forces, 0)
    for index in range(tiles):
        x, y, z = tile_of(index, OWN)
        for comp in range(3):
            forces_ref[comp, x, y, z : z + 1, :] = results[index, comp : comp + 1, :]
        energy_ref[x, y, z : z + 1, :] = results[index, 3:4, :]


def shards(sizes, positions, species, counts):
    vmem = pl.BlockSpec(memory_space=pltpu.VMEM)
    smem = pl.BlockSpec(memory_space=pltpu.SMEM)
    tiles = OWN[0] * OWN[1] * OWN[2]
    full, embed, near, held = pl.pallas_call(
        lambda *refs: exchange_kernel(sizes, *refs),
        name="exchange",
        out_shape=(
            jax.ShapeDtypeStruct(EXT + (8, TILE), F32),
            jax.ShapeDtypeStruct((tiles, 1, TILE), F32),
            jax.ShapeDtypeStruct((tiles, 32, TILE), jnp.int32),
            jax.ShapeDtypeStruct((1, tiles * 32), jnp.int32),
        ),
        in_specs=[vmem, vmem, smem],
        out_specs=(vmem, vmem, vmem, vmem),
        scratch_shapes=[
            pltpu.VMEM(EXT + (4, TILE), F32),
            pltpu.VMEM(EXT + (1, TILE), F32),
            pltpu.VMEM((EXT[0] * EXT[1], 48, EXT[2] * TILE), BF16),
            pltpu.VMEM((tiles, TILE, 48), BF16),
            pltpu.VMEM((tiles, TILE, TILE), F32),
            pltpu.VMEM((tiles, 32, TILE), F32),
            pltpu.SemaphoreType.DMA((2, len(OFFSETS))),
            pltpu.SemaphoreType.DMA((2, len(OFFSETS))),
        ],
        compiler_params=pltpu.CompilerParams(collective_id=0, has_side_effects=True),
    )(positions, species, counts)
    return pl.pallas_call(
        force_kernel,
        name="forces",
        out_shape=(
            jax.ShapeDtypeStruct((3,) + OWN + (TILE,), F32),
            jax.ShapeDtypeStruct(OWN + (TILE,), F32),
        ),
        in_specs=[vmem, vmem, vmem, smem],
        out_specs=(vmem, vmem),
        scratch_shapes=[
            pltpu.VMEM((tiles, 32 + GROUP, 8, TILE), F32),
            pltpu.VMEM((TILE, TILE), F32),
            pltpu.VMEM((tiles, 8, TILE), F32),
            pltpu.SMEM((tiles,), jnp.int32),
        ],
    )(full, embed, near, held)


def solution(mesh):
    placed = (P(None, "gx", "gy", "gz", None), P("gx", "gy", "gz", None), P("gx", "gy", "gz"))
    sizes = tuple(mesh.shape[name] for name in ("gx", "gy", "gz"))
    return jax.shard_map(
        lambda *args: shards(sizes, *args),
        mesh=mesh,
        in_specs=placed,
        out_specs=(P(None, "gx", "gy", "gz", None), P("gx", "gy", "gz", None)),
        check_vma=False,
    )
```

time: 73.2 us -> 50.4 us (0.69)
  Pallas kernels: 69.4 us -> 49.4 us
  local copies, waits for them, and re-layouts: 2.9 us -> 0 us
    pallas_call x1, Pallas kernels: 27.5 us -> 14 us  [shards(): pl.pallas_call(force_kernel, name='forces', out_shape=(jax.ShapeDtypeStru...]
    pallas_call x1, Pallas kernels: 41.9 us -> 35.4 us  [shards(): pl.pallas_call(lambda *refs: exchange_kernel(sizes, *refs), name='exchang...]
    slice x2 -> x0, local copies, waits for them, and re-layouts: 2.29 us -> none  [shards(): return (jnp.moveaxis(result[..., :3, :], 3, 0), result[..., 3, :])]
where the time goes in v2:
time: 50.4 us; the launch traced here: 50.1 us
  Pallas kernels  49.4 us (98%)
  between operations  0.64 us (1%)
    pallas_call x1, Pallas kernels, shards(): pl.pallas_call(lambda *refs: exchange_kernel(sizes, *refs), name='exchang...  35.4 us
    pallas_call x1, Pallas kernels, shards(): pl.pallas_call(force_kernel, name='forces', out_shape=(jax.ShapeDtypeStru...  14 us

profile of v2, /device:TPU:1, one launch (start us, length us, event | category | flops | bytes accessed | tf_op | source)
XLA Modules:
  0.0 50.1 jit_solution(1507118913516218016)
XLA Ops:
  0.6 35.4 %exchange.1 = (f32[4,4,6,8,128]{4,3,2,1,0:T(8,128)}, f32[16,1,128]{2,1,0:T(1,128)}, s32[16,32,128]{2,1,0:T(8,128)}, s32[1,512]{1,0:T(1,128)}) custom-call(f32[3,2,2,4,128]{4,3,2,1,0:T(4,128)} %refs_0_.1, s32[2,2,4,128]{3,2,1,0:T(4,128)} %refs_1_.1, s32[2,2,4]{2,1,0:T(2,128)} %refs_2_.1), custom_call_target="tpu_custom_call" | custom-call | tf_op jit(solution)/shard_map/exchange/pallas_call | solution.py:425
  36.1 14.0 %forces.1 = (f32[3,2,2,4,128]{4,3,2,1,0:T(4,128)}, f32[2,2,4,128]{3,2,1,0:T(4,128)}) custom-call(f32[4,4,6,8,128]{4,3,2,1,0:T(8,128)} %get-tuple-element.6.full_ref, f32[16,1,128]{2,1,0:T(1,128)} %get-tuple-element.7.embed_ref, s32[16,32,128]{2,1,0:T(8,128)} %get-tuple-element.8.near_ref, s32[1,512]{1,0:T(1,128)} %get-tuple-element.9.held_ref), custom_call_target="tpu_custom_call" | custom-call | tf_op jit(solution)/shard_map/forces/pallas_call | solution.py:448

commit v3 on v2

--- a/solution.py
+++ b/solution.py
@@ -22,6 +22,8 @@
 BETA = -4.0 / CUTOFF_SQUARED * 0.09
 SLOPE = ALPHA / (5.0 * BETA)
 PART = 128
+TILES = OWN[0] * OWN[1] * OWN[2]
+UNROLL = 4
 FORCE_PART = 64
 GROUP = 6
 HIGHEST = lax.Precision.HIGHEST
@@ -79,13 +81,16 @@
     full_ref,
     embed_ref,
     near_ref,
-    held_ref,
+    begin_ref,
+    used_ref,
     wire,
     slope,
     beside,
     own,
     totals,
     reach_rows,
+    weights,
+    columns_ref,
     sends,
     recvs,
 ):
@@ -111,6 +116,8 @@
                 for comp in range(3):
                     value = jnp.where(row4 == comp, pos_ref[comp, x, y, z : z + 1, :], value)
                 wire[x + 1, y + 1, z + 1] = value
+                index = (x * OWN[1] + y) * OWN[2] + z
+                weights[index : index + 1, :] = weight
     pl.semaphore_wait(barrier, len(OFFSETS))
 
     def copies(ref, which):
@@ -178,7 +185,7 @@
 
     parts = TILE // PART
 
-    def inner(index, _):
+    def inner_tile(index):
         x, y, z = tile_of(index, OWN)
         for part in range(parts):
             cut = slice(part * PART, (part + 1) * PART)
@@ -196,9 +203,13 @@
                     else:
                         total = total + blocks(cube)
             totals[index, cut] = total
-        return _
-
-    lax.fori_loop(0, OWN[0] * OWN[1] * OWN[2], inner, 0)
+
+    def inner(step, _):
+        for k in range(UNROLL):
+            inner_tile(step * UNROLL + k)
+        return _
+
+    lax.fori_loop(0, TILES // UNROLL, inner, 0)
 
     for copy in state_copies:
         copy.wait()
@@ -218,8 +229,6 @@
         return _
 
     lax.fori_loop(0, OWN[0] * OWN[1], prepare_ends, 0)
-
-    ones = jnp.ones((8, TILE), F32)
 
     def ends(index, _):
         column, upper = index // 2, lax.rem(index, 2)
@@ -237,29 +246,35 @@
 
     lax.fori_loop(0, 2 * OWN[0] * OWN[1], ends, 0)
 
-    def outer(index, _):
+    lanes = lax.broadcasted_iota(jnp.int32, (TILE, TILE), 1)
+
+    def outer_tile(index):
         x, y, z = tile_of(index, OWN)
         side_x, side_y = x * (EXT[0] - 1), y * (EXT[1] - 1)
         columns = [side_x * EXT[1] + y + dy for dy in range(3)]
         columns += [(dx + 1) * EXT[1] + side_y for dx in range(OWN[0])]
-        for part in range(parts):
-            cut = slice(part * PART, (part + 1) * PART)
-            rows = own[index, cut]
-            total = totals[index, cut]
-            for column in columns:
-                total = total + blocks(cubes(rows, window(column, z)))
-            totals[index, cut] = total
-        result = lax.dot_general(
-            ones, totals[index], NT, precision=HIGHEST, preferred_element_type=F32
-        )
-        root = jnp.sqrt(1.0 + result[0:1])
-        weight = wire[x + 1, y + 1, z + 1, 3:4, :]
-        strength = jnp.where(weight > 6.0, 0.7, jnp.where(weight > 0.0, 1.0, 0.0))
-        embed_ref[index] = -strength * root
-        slope[x + 1, y + 1, z + 1] = -0.5 * SLOPE * strength / root
-        return _
-
-    lax.fori_loop(0, OWN[0] * OWN[1] * OWN[2], outer, 0)
+        total = totals[index]
+        for column in columns:
+            total = total + blocks(cubes(own[index], window(column, z)))
+        return jnp.sum(total, axis=1, keepdims=True)
+
+    def outer(step, _):
+        value = columns_ref[...]
+        for k in range(UNROLL):
+            index = step * UNROLL + k
+            value = jnp.where(lanes == index, outer_tile(index), value)
+        columns_ref[...] = value
+        return _
+
+    lax.fori_loop(0, TILES // UNROLL, outer, 0)
+    root = jnp.sqrt(1.0 + columns_ref[...].T[:TILES])
+    weight = weights[...]
+    strength = jnp.where(weight > 6.0, 0.7, jnp.where(weight > 0.0, 1.0, 0.0))
+    embed_ref[...] = -strength * root
+    rows = -0.5 * SLOPE * strength / root
+    for index in range(TILES):
+        x, y, z = tile_of(index, OWN)
+        slope[x + 1, y + 1, z + 1] = rows[index : index + 1]
 
     slope_copies = copies(slope, 1)
     for copy in slope_copies:
@@ -286,22 +301,35 @@
     first = lax.broadcasted_iota(jnp.int32, (TILE, TILE), 0)
     second = lax.broadcasted_iota(jnp.int32, (TILE, TILE), 1)
     earlier = (first < second).astype(F32).astype(BF16)
+    ones = jnp.ones((TILE, TILE), BF16)
+    above_rows = ((second < first) & (second // 32 == first // 32)).astype(F32).astype(BF16)
+    first_lane = (lax.broadcasted_iota(jnp.int32, (8, TILE), 1) == 0).astype(F32).astype(BF16)
 
     def compress(group, _):
         rows = reach_rows[pl.ds(group * 4, 4)].reshape(TILE, TILE)
         near = rows < CUTOFF_SQUARED * 1.00002
         flags = near.astype(F32).astype(BF16)
         before = jnp.dot(flags, earlier, preferred_element_type=F32).astype(jnp.int32)
+        held = jnp.dot(flags, ones, preferred_element_type=F32).astype(BF16)
+        filled = jnp.dot(above_rows, held, preferred_element_type=F32).astype(jnp.int32)
         word = jnp.where(near, 16384 + second * 128 + (second - before), 0)
         for bit in range(7):
             moved = pltpu.roll(word, TILE - (1 << bit), 1)
             stay = jnp.where((word & (1 << bit)) != 0, 0, word)
             word = jnp.where((moved & (1 << bit)) != 0, moved, stay)
-        near_ref[pl.ds(group * 4, 4)] = ((word >> 7) & 127).reshape(4, 32, TILE)
-        held = lax.dot_general(
-            jnp.ones((8, TILE), BF16), flags, NT, preferred_element_type=F32
-        )
-        held_ref[:, pl.ds(pl.multiple_of(group * TILE, TILE), TILE)] = held[0:1].astype(jnp.int32)
+        for bit in range(7):
+            word = jnp.where((filled & (1 << bit)) != 0, pltpu.roll(word, 1 << bit, 1), word)
+        start = filled & (TILE - 1)
+        code = ((word >> 7) & 127) + jnp.where(second < start, TILE, 0)
+        near_ref[pl.ds(group * 4, 4)] = jnp.where(word >= 16384, code, 512).reshape(4, 32, TILE)
+        cut = pl.ds(pl.multiple_of(group * TILE, TILE), TILE)
+        for ref, value in (
+            (begin_ref, 1 + (filled >> 7)),
+            (used_ref, 1 + ((filled + TILE - 1) >> 7)),
+        ):
+            value = value.astype(F32).astype(BF16)
+            value = lax.dot_general(first_lane, value, NT, preferred_element_type=F32)
+            ref[:, cut] = value[0:1].astype(jnp.int32)
         return _
 
     lax.fori_loop(0, 4, compress, 0)
@@ -322,117 +350,128 @@
 
 
 def force_kernel(
-    full_ref, embed_ref, near_ref, held_ref, forces_ref, energy_ref, packed, sums, results, total_ref
+    full_ref, embed_ref, near_ref, begin_ref, used_ref, forces_ref, energy_ref, packed, sums, results
 ):
     row = lax.broadcasted_iota(jnp.int32, (8, TILE), 0)
-    lane = lax.broadcasted_iota(jnp.int32, (8, TILE), 1)
-    masks = ((row < 3) | (row == 4) | (row == 5), (row == 3) | (row == 6), row == 7)
-    tiles = OWN[0] * OWN[1] * OWN[2]
-
-    def pack(index, _):
+
+    def pack_tile(index):
         x, y, z = tile_of(index, OWN)
         packed[index, 0] = full_ref[x + 1, y + 1, z + 1]
-        filled = 0
         current = jnp.zeros((8, TILE), F32)
+        chunk = begin_ref[0, index * 32]
         for k, offset in enumerate(OFFSETS):
-            held = held_ref[0, index * 32 + k]
             there = full_ref[tuple(a + 1 + o for a, o in zip((x, y, z), offset))]
-            places = jnp.broadcast_to(near_ref[index, k : k + 1, :], (8, TILE))
+            code = jnp.broadcast_to(near_ref[index, k : k + 1, :], (8, TILE))
+            places = code & (TILE - 1)
             value = jnp.take_along_axis(there, places, axis=1, mode="promise_in_bounds")
-            value = jnp.where(lane < held, value, 0.0)
-            start = filled & (TILE - 1)
-            value = pltpu.roll(value, start, 1)
-            behind = lane >= start
-            merged = jnp.where(behind, value, current)
-            beyond = jnp.where(behind, 0.0, value)
-            chunk = 1 + (filled >> 7)
+            merged = jnp.where(code < TILE, value, current)
+            beyond = jnp.where((code & TILE) != 0, value, 0.0)
             packed[index, chunk] = merged
             packed[index, chunk + 1] = beyond
-            filled = filled + held
-            current = jnp.where((filled >> 7) + 1 > chunk, beyond, merged)
-        for k in range(GROUP):
-            packed[index, 2 + (filled >> 7) + k] = jnp.zeros((8, TILE), F32)
-        total_ref[index] = filled
-        return _
-
-    lax.fori_loop(0, tiles, pack, 0)
-
-    def group(index, own, start, count, with_self):
-        lanes = lax.broadcasted_iota(jnp.int32, (FORCE_PART, TILE), 1)
+            later = begin_ref[0, index * 32 + k + 1]
+            current = jnp.where(later > chunk, beyond, merged)
+            chunk = later
+        for k in range(1, GROUP + 1):
+            packed[index, chunk + k] = jnp.zeros((8, TILE), F32)
+
+    def pack(step, _):
+        for k in range(UNROLL):
+            pack_tile(step * UNROLL + k)
+        return _
+
+    lax.fori_loop(0, TILES // UNROLL, pack, 0)
+
+    def group(index, own, start, count, with_self, room):
+        shape = (FORCE_PART, TILE)
+        lanes = lax.broadcasted_iota(jnp.int32, shape, 1)
         values = [packed[index, start + k] for k in range(count)]
         features = [
-            [beside_features(jnp.where(mask, value, 0.0)) for mask in masks] for value in values
+            jnp.concatenate([beside_features(value) for value in values[k : k + 2]], axis=1)
+            for k in range(0, count, 2)
         ]
         for part in range(TILE // FORCE_PART):
-            rows = own[part * FORCE_PART : (part + 1) * FORCE_PART]
-            total = [jnp.zeros((FORCE_PART, TILE), F32) for _ in range(5)]
-            for k, value in enumerate(values):
-                reach, both, pair = (
-                    jnp.dot(rows, feature, preferred_element_type=F32) for feature in features[k]
-                )
-                q = jnp.maximum(reach, 0.0)
-                if with_self and k == 0:
-                    here = lax.broadcasted_iota(jnp.int32, (FORCE_PART, TILE), 0) + part * FORCE_PART
-                    q = jnp.where(here == lanes, 0.0, q)
-                square = q * q
-                pull = square * (q * pair)
-                coef = pull + square * both
-                for comp in range(3):
-                    total[comp] = total[comp] + coef * value[comp : comp + 1]
-                total[3] = total[3] + coef
-                total[4] = total[4] + pull * q
-            column = jnp.zeros((FORCE_PART, TILE), F32)
+            cut = slice(part * FORCE_PART, (part + 1) * FORCE_PART)
+            total = [jnp.zeros(shape, F32) for _ in range(5)]
+            for pair_index, feature in enumerate(features):
+                products = [
+                    jnp.dot(rows[cut], feature, preferred_element_type=F32) for rows in own
+                ]
+                for side in range(2):
+                    k = 2 * pair_index + side
+                    value = values[k]
+                    reach, both, pair = (
+                        product[:, side * TILE : (side + 1) * TILE] for product in products
+                    )
+                    q = jnp.maximum(reach, 0.0)
+                    if with_self and k == 0:
+                        here = lax.broadcasted_iota(jnp.int32, shape, 0) + part * FORCE_PART
+                        q = jnp.where(here == lanes, 0.0, q)
+                    square = q * q
+                    pull = square * (q * pair)
+                    coef = pull + square * both
+                    for comp in range(3):
+                        total[comp] = total[comp] + coef * value[comp : comp + 1]
+                    total[3] = total[3] + coef
+                    total[4] = total[4] + pull * q
+            column = jnp.zeros(shape, F32)
             for k in range(5):
                 column = jnp.where(lanes == k, jnp.sum(total[k], axis=1, keepdims=True), column)
-            sums[part * FORCE_PART : (part + 1) * FORCE_PART, :] = column
-        return sums[...].T[:8]
+            sums[room, cut, :] = column
+        return sums[room].T[:8]
 
     def own_rows(value):
         out = jnp.where(row == 3, value[6:7], value)
         out = jnp.where(row == 4, 1.0 + value[5:6], out)
         out = jnp.where(row == 5, 1.0, out)
-        return own_features(jnp.where(row == 6, value[3:4], out))
-
-    def forces(index, _):
-        value = packed[index, 0]
-        own = own_rows(value)
-        chunks = 1 + ((total_ref[index] + TILE - 1) >> 7)
-        result = group(index, own, 0, GROUP, True)
-        more = (chunks - GROUP + 1) // 2
-        result = lax.fori_loop(
-            0,
-            jnp.maximum(more, 0),
-            lambda step, carry: carry + group(index, own, GROUP + 2 * step, 2, False),
-            result,
-        )
-        moved = (2.0 * BETA / SCALE) * (result - value * result[3:4])
-        energy = embed_ref[index] + (0.5 * 0.09) * result[4:5]
-        results[index] = jnp.where(row == 3, energy, moved)
-        return _
-
-    lax.fori_loop(0, tiles, forces, 0)
-    for index in range(tiles):
+        a, b, c = pieces(jnp.where(row == 6, value[3:4], out))
+        columns = jnp.concatenate([a, a, b, b, a, c], axis=0).T
+        place = lax.broadcasted_iota(jnp.int32, columns.shape, 1) % 8
+        masks = ((place < 3) | (place == 4) | (place == 5), (place == 3) | (place == 6), place == 7)
+        return [jnp.where(mask, columns, 0.0).astype(BF16) for mask in masks]
+
+    def forces(step, _):
+        done = []
+        for k in range(UNROLL):
+            index = step * UNROLL + k
+            own = own_rows(packed[index, 0])
+            done.append((index, own, group(index, own, 0, GROUP, True, k)))
+        for k, (index, own, result) in enumerate(done):
+            results[index] = result
+            more = (used_ref[0, index * 32 + 31] - GROUP + 1) // 2
+
+            def further(extra, _, index=index, own=own, k=k):
+                results[index] += group(index, own, GROUP + 2 * extra, 2, False, k)
+                return _
+
+            lax.fori_loop(0, jnp.maximum(more, 0), further, 0)
+        return _
+
+    lax.fori_loop(0, TILES // UNROLL, forces, 0)
+    for index in range(TILES):
         x, y, z = tile_of(index, OWN)
+        result = results[index]
+        moved = (2.0 * BETA / SCALE) * (result - packed[index, 0] * result[3:4])
         for comp in range(3):
-            forces_ref[comp, x, y, z : z + 1, :] = results[index, comp : comp + 1, :]
-        energy_ref[x, y, z : z + 1, :] = results[index, 3:4, :]
+            forces_ref[comp, x, y, z : z + 1, :] = moved[comp : comp + 1]
+        energy_ref[x, y, z : z + 1, :] = embed_ref[index : index + 1] + 0.045 * result[4:5]
 
 
 def shards(sizes, positions, species, counts):
     vmem = pl.BlockSpec(memory_space=pltpu.VMEM)
     smem = pl.BlockSpec(memory_space=pltpu.SMEM)
     tiles = OWN[0] * OWN[1] * OWN[2]
-    full, embed, near, held = pl.pallas_call(
+    full, embed, near, begin, used = pl.pallas_call(
         lambda *refs: exchange_kernel(sizes, *refs),
         name="exchange",
         out_shape=(
             jax.ShapeDtypeStruct(EXT + (8, TILE), F32),
-            jax.ShapeDtypeStruct((tiles, 1, TILE), F32),
+            jax.ShapeDtypeStruct((tiles, TILE), F32),
             jax.ShapeDtypeStruct((tiles, 32, TILE), jnp.int32),
+            jax.ShapeDtypeStruct((1, tiles * 32), jnp.int32),
             jax.ShapeDtypeStruct((1, tiles * 32), jnp.int32),
         ),
         in_specs=[vmem, vmem, smem],
-        out_specs=(vmem, vmem, vmem, vmem),
+        out_specs=(vmem,) * 5,
         scratch_shapes=[
             pltpu.VMEM(EXT + (4, TILE), F32),
             pltpu.VMEM(EXT + (1, TILE), F32),
@@ -440,10 +479,12 @@
             pltpu.VMEM((tiles, TILE, 48), BF16),
             pltpu.VMEM((tiles, TILE, TILE), F32),
             pltpu.VMEM((tiles, 32, TILE), F32),
+            pltpu.VMEM((tiles, TILE), F32),
+            pltpu.VMEM((TILE, TILE), F32),
             pltpu.SemaphoreType.DMA((2, len(OFFSETS))),
             pltpu.SemaphoreType.DMA((2, len(OFFSETS))),
         ],
-        compiler_params=pltpu.CompilerParams(collective_id=0, has_side_effects=True),
+        compiler_params=pltpu.CompilerParams(collective_id=0, has_side_effects=True, vmem_limit_bytes=24 << 20),
     )(positions, species, counts)
     return pl.pallas_call(
         force_kernel,
@@ -452,15 +493,15 @@
             jax.ShapeDtypeStruct((3,) + OWN + (TILE,), F32),
             jax.ShapeDtypeStruct(OWN + (TILE,), F32),
         ),
-        in_specs=[vmem, vmem, vmem, smem],
+        in_specs=[vmem, vmem, vmem, smem, smem],
         out_specs=(vmem, vmem),
         scratch_shapes=[
             pltpu.VMEM((tiles, 32 + GROUP, 8, TILE), F32),
-            pltpu.VMEM((TILE, TILE), F32),
+            pltpu.VMEM((UNROLL, TILE, TILE), F32),
             pltpu.VMEM((tiles, 8, TILE), F32),
-            pltpu.SMEM((tiles,), jnp.int32),
         ],
-    )(full, embed, near, held)
+        compiler_params=pltpu.CompilerParams(vmem_limit_bytes=24 << 20),
+    )(full, embed, near, begin, used)
 
 
 def solution(mesh):

time: 50.4 us -> 40.6 us (0.81)
  Pallas kernels: 49.4 us -> 37.6 us
  local copies, waits for them, and re-layouts: 0 us -> 2.11 us
    pallas_call x1, Pallas kernels: 35.4 us -> 29.5 us  [shards(): pl.pallas_call(lambda *refs: exchange_kernel(sizes, *refs), name='exchang...]
    pallas_call x1, Pallas kernels: 14 us -> 8.14 us  [shards(): pl.pallas_call(force_kernel, name='forces', out_shape=(jax.ShapeDtypeStru...]
    unnamed x0 -> x6, local copies, waits for them, and re-layouts: none -> 2.11 us
where the time goes in v3:
time: 40.6 us; the launch traced here: 40.4 us
  Pallas kernels  37.6 us (93%)
  local copies, waits for them, and re-layouts  2.11 us (5%)
  between operations  0.65 us (2%)
    pallas_call x1, Pallas kernels, shards(): pl.pallas_call(lambda *refs: exchange_kernel(sizes, *refs), name='exchang...  29.5 us
    pallas_call x1, Pallas kernels, shards(): pl.pallas_call(force_kernel, name='forces', out_shape=(jax.ShapeDtypeStru...  8.14 us
    unnamed x6, local copies, waits for them, and re-layouts  2.11 us

profile of v3, /device:TPU:1, one launch (start us, length us, event | category | flops | bytes accessed | tf_op | source)
XLA Modules:
  0.0 40.4 jit_solution(17301885815640126797)
XLA Ops:
  0.6 0.0 copy-start
  0.6 0.7 %copy-done = f32[3,2,2,4,128]{4,3,2,1,0:T(4,128)S(1)} copy-done((f32[3,2,2,4,128]{4,3,2,1,0:T(4,128)S(1)}, f32[3,2,2,4,128]{4,3,2,1,0:T(4,128)}, u32[]{:S(2)}) %copy-start) | copy-done | bytes 24600
  1.4 0.0 copy-start.1
  1.4 0.7 %copy-done.1 = s32[2,2,4,128]{3,2,1,0:T(4,128)S(1)} copy-done((s32[2,2,4,128]{3,2,1,0:T(4,128)S(1)}, s32[2,2,4,128]{3,2,1,0:T(4,128)}, u32[]{:S(2)}) %copy-start.1) | copy-done | bytes 8216
  2.1 0.0 copy-start.2
  2.1 0.7 %copy-done.2 = s32[2,2,4]{2,1,0:T(2,128)S(1)} copy-done((s32[2,2,4]{2,1,0:T(2,128)S(1)}, s32[2,2,4]{2,1,0:T(2,128)}, u32[]{:S(2)}) %copy-start.2) | copy-done | bytes 88
  2.7 29.5 %exchange.1 = (f32[4,4,6,8,128]{4,3,2,1,0:T(8,128)S(1)}, f32[16,128]{1,0:T(8,128)S(1)}, s32[16,32,128]{2,1,0:T(8,128)S(1)}, s32[1,512]{1,0:T(1,128)S(1)}, s32[1,512]{1,0:T(1,128)S(1)}) custom-call(f32[3,2,2,4,128]{4,3,2,1,0:T(4,128)S(1)} %copy-done, s32[2,2,4,128]{3,2,1,0:T(4,128)S(1)} %copy-done.1, s32[2,2,4]{2,1,0:T(2,128)S(1)} %copy-done.2), custom_call_target="tpu_custom_call" | custom-call | tf_op jit(solution)/shard_map/exchange/pallas_call | solution.py:463
  32.2 8.1 %forces.1 = (f32[3,2,2,4,128]{4,3,2,1,0:T(4,128)}, f32[2,2,4,128]{3,2,1,0:T(4,128)}) custom-call(f32[4,4,6,8,128]{4,3,2,1,0:T(8,128)S(1)} %get-tuple-element.7.full_ref, f32[16,128]{1,0:T(8,128)S(1)} %get-tuple-element.8.embed_ref, s32[16,32,128]{2,1,0:T(8,128)S(1)} %get-tuple-element.9.near_ref, s32[1,512]{1,0:T(1,128)S(1)} %get-tuple-element.10.begin_ref, ...), custom_call_target="tpu_custom_call" | custom-call | tf_op jit(solution)/shard_map/forces/pallas_call | solution.py:489
Async XLA Ops:
  0.6 0.7 %copy-start = (f32[3,2,2,4,128]{4,3,2,1,0:T(4,128)S(1)}, f32[3,2,2,4,128]{4,3,2,1,0:T(4,128)}, u32[]{:S(2)}) copy-start(f32[3,2,2,4,128]{4,3,2,1,0:T(4,128)} %refs_0_.1) | copy-start | bytes 73732
  1.4 0.7 %copy-start.1 = (s32[2,2,4,128]{3,2,1,0:T(4,128)S(1)}, s32[2,2,4,128]{3,2,1,0:T(4,128)}, u32[]{:S(2)}) copy-start(s32[2,2,4,128]{3,2,1,0:T(4,128)} %refs_1_.1) | copy-start | bytes 24580
  2.1 0.7 %copy-start.2 = (s32[2,2,4]{2,1,0:T(2,128)S(1)}, s32[2,2,4]{2,1,0:T(2,128)}, u32[]{:S(2)}) copy-start(s32[2,2,4]{2,1,0:T(2,128)} %refs_2_.1) | copy-start | bytes 196

commit v4 on v3

--- a/solution.py
+++ b/solution.py
@@ -15,9 +15,10 @@
 TILE = 128
 OWN = (2, 2, 4)
 EXT = (4, 4, 6)
-OFFSETS = [
-    (a, b, c) for a in (-1, 0, 1) for b in (-1, 0, 1) for c in (-1, 0, 1) if (a, b, c) != (0, 0, 0)
-]
+OFFSETS = sorted(
+    [(a, b, c) for a in (-1, 0, 1) for b in (-1, 0, 1) for c in (-1, 0, 1) if a or b or c],
+    key=lambda offset: -sum(map(abs, offset)),
+)
 ALPHA = -3.0 / CUTOFF_SQUARED
 BETA = -4.0 / CUTOFF_SQUARED * 0.09
 SLOPE = ALPHA / (5.0 * BETA)
@@ -75,9 +76,9 @@
 
 def exchange_kernel(
     sizes,
-    pos_ref,
-    spec_ref,
-    count_ref,
+    pos_hbm,
+    spec_hbm,
+    count_hbm,
     full_ref,
     embed_ref,
     near_ref,
@@ -91,9 +92,21 @@
     reach_rows,
     weights,
     columns_ref,
+    pos_ref,
+    spec_ref,
+    count_ref,
+    loads,
     sends,
     recvs,
 ):
+    arrivals = [
+        pltpu.make_async_copy(source, target, loads.at[k])
+        for k, (source, target) in enumerate(
+            ((count_hbm, count_ref), (pos_hbm, pos_ref), (spec_hbm, spec_ref))
+        )
+    ]
+    for copy in arrivals:
+        copy.start()
     me = [lax.axis_index(name) for name in ("gx", "gy", "gz")]
 
     def peer(offset):
@@ -103,6 +116,8 @@
     for offset in OFFSETS:
         pl.semaphore_signal(barrier, inc=1, device_id=peer(offset), device_id_type=MESH)
 
+    for copy in arrivals:
+        copy.wait()
     lane = lax.broadcasted_iota(jnp.int32, (1, TILE), 1)
     row4 = lax.broadcasted_iota(jnp.int32, (4, TILE), 0)
     for x in range(OWN[0]):
@@ -212,7 +227,7 @@
     lax.fori_loop(0, TILES // UNROLL, inner, 0)
 
     for copy in state_copies:
-        copy.wait()
+        copy.wait_recv()
 
     def prepare_side(index, _):
         x = jnp.where(index < 4, 0, jnp.where(index < 8, EXT[0] - 1, 1 + (index - 8) // 2))
@@ -230,7 +245,7 @@
 
     lax.fori_loop(0, OWN[0] * OWN[1], prepare_ends, 0)
 
-    def ends(index, _):
+    def ends_tile(index):
         column, upper = index // 2, lax.rem(index, 2)
         tile = column * OWN[2] + upper * (OWN[2] - 1)
         for part in range(parts):
@@ -242,9 +257,13 @@
                     there = (x + 1) * EXT[1] + y + 1
                     total = total + cubes(rows, window(there, upper * (EXT[2] - 1), 1))
             totals[tile, cut] = total
-        return _
-
-    lax.fori_loop(0, 2 * OWN[0] * OWN[1], ends, 0)
+
+    def ends(step, _):
+        for k in range(UNROLL):
+            ends_tile(step * UNROLL + k)
+        return _
+
+    lax.fori_loop(0, 2 * OWN[0] * OWN[1] // UNROLL, ends, 0)
 
     lanes = lax.broadcasted_iota(jnp.int32, (TILE, TILE), 1)
 
@@ -334,8 +353,10 @@
 
     lax.fori_loop(0, 4, compress, 0)
 
+    for copy in state_copies:
+        copy.wait_send()
     for copy in slope_copies:
-        copy.wait()
+        copy.wait_recv()
 
     def finish(index, _):
         for z in range(EXT[2]):
@@ -347,6 +368,8 @@
         return _
 
     lax.fori_loop(0, EXT[0] * EXT[1], finish, 0)
+    for copy in slope_copies:
+        copy.wait_send()
 
 
 def force_kernel(
@@ -470,7 +493,7 @@
             jax.ShapeDtypeStruct((1, tiles * 32), jnp.int32),
             jax.ShapeDtypeStruct((1, tiles * 32), jnp.int32),
         ),
-        in_specs=[vmem, vmem, smem],
+        in_specs=[pl.BlockSpec(memory_space=pltpu.HBM)] * 3,
         out_specs=(vmem,) * 5,
         scratch_shapes=[
             pltpu.VMEM(EXT + (4, TILE), F32),
@@ -481,11 +504,15 @@
             pltpu.VMEM((tiles, 32, TILE), F32),
             pltpu.VMEM((tiles, TILE), F32),
             pltpu.VMEM((TILE, TILE), F32),
+            pltpu.VMEM((3,) + OWN + (TILE,), F32),
+            pltpu.VMEM(OWN + (TILE,), jnp.int32),
+            pltpu.SMEM(OWN, jnp.int32),
+            pltpu.SemaphoreType.DMA((3,)),
             pltpu.SemaphoreType.DMA((2, len(OFFSETS))),
             pltpu.SemaphoreType.DMA((2, len(OFFSETS))),
         ],
         compiler_params=pltpu.CompilerParams(collective_id=0, has_side_effects=True, vmem_limit_bytes=24 << 20),
-    )(positions, species, counts)
+    )(*(pltpu.with_memory_space_constraint(a, pltpu.HBM) for a in (positions, species, counts)))
     return pl.pallas_call(
         force_kernel,
         name="forces",

time: 40.6 us -> 36.3 us (0.89)
  local copies, waits for them, and re-layouts: 2.11 us -> 0 us
  Pallas kernels: 37.6 us -> 35.6 us
    unnamed x6 -> x0, local copies, waits for them, and re-layouts: 2.11 us -> none
    pallas_call x1, Pallas kernels: 29.5 us -> 27.4 us  [shards(): pl.pallas_call(lambda *refs: exchange_kernel(sizes, *refs), name='exchang...]
where the time goes in v4:
time: 36.3 us; the launch traced here: 36.2 us
  Pallas kernels  35.6 us (98%)
  between operations  0.64 us (2%)
    pallas_call x1, Pallas kernels, shards(): pl.pallas_call(lambda *refs: exchange_kernel(sizes, *refs), name='exchang...  27.4 us
    pallas_call x1, Pallas kernels, shards(): pl.pallas_call(force_kernel, name='forces', out_shape=(jax.ShapeDtypeStru...  8.14 us

profile of v4, /device:TPU:1, one launch (start us, length us, event | category | flops | bytes accessed | tf_op | source)
XLA Modules:
  0.0 36.2 jit_solution(5058482741642869680)
XLA Ops:
  0.6 27.4 %exchange.1 = (f32[4,4,6,8,128]{4,3,2,1,0:T(8,128)S(1)}, f32[16,128]{1,0:T(8,128)S(1)}, s32[16,32,128]{2,1,0:T(8,128)S(1)}, s32[1,512]{1,0:T(1,128)S(1)}, s32[1,512]{1,0:T(1,128)S(1)}) custom-call(f32[3,2,2,4,128]{4,3,2,1,0:T(4,128)} %refs_0_.1, s32[2,2,4,128]{3,2,1,0:T(4,128)} %refs_1_.1, s32[2,2,4]{2,1,0:T(2,128)} %refs_2_.1), custom_call_target="tpu_custom_call" | custom-call | tf_op jit(solution)/shard_map/exchange/pallas_call | solution.py:486
  28.1 8.1 %forces.1 = (f32[3,2,2,4,128]{4,3,2,1,0:T(4,128)}, f32[2,2,4,128]{3,2,1,0:T(4,128)}) custom-call(f32[4,4,6,8,128]{4,3,2,1,0:T(8,128)S(1)} %get-tuple-element.7.full_ref, f32[16,128]{1,0:T(8,128)S(1)} %get-tuple-element.8.embed_ref, s32[16,32,128]{2,1,0:T(8,128)S(1)} %get-tuple-element.9.near_ref, s32[1,512]{1,0:T(1,128)S(1)} %get-tuple-element.10.begin_ref, ...), custom_call_target="tpu_custom_call" | custom-call | tf_op jit(solution)/shard_map/forces/pallas_call | solution.py:516

commit v5 on v4

--- a/solution.py
+++ b/solution.py
@@ -140,13 +140,17 @@
             pltpu.make_async_remote_copy(
                 src_ref=ref.at[region(offset, True)],
                 dst_ref=ref.at[region(offset, False)],
-                send_sem=sends.at[which, k],
-                recv_sem=recvs.at[which, k],
+                send_sem=sends.at[which],
+                recv_sem=recvs.at[which],
                 device_id=peer(offset),
                 device_id_type=MESH,
             )
-            for k, offset in enumerate(OFFSETS)
+            for offset in OFFSETS
         ]
+
+    def settle(ref, sems, which):
+        whole = ref.at[:, :, 0 : EXT[2] - 1]
+        pltpu.make_async_copy(whole, whole, sems.at[which]).wait()
 
     state_copies = copies(wire, 0)
     for copy in state_copies:
@@ -226,8 +230,7 @@
 
     lax.fori_loop(0, TILES // UNROLL, inner, 0)
 
-    for copy in state_copies:
-        copy.wait_recv()
+    settle(wire, recvs, 0)
 
     def prepare_side(index, _):
         x = jnp.where(index < 4, 0, jnp.where(index < 8, EXT[0] - 1, 1 + (index - 8) // 2))
@@ -277,29 +280,40 @@
             total = total + blocks(cubes(own[index], window(column, z)))
         return jnp.sum(total, axis=1, keepdims=True)
 
-    def outer(step, _):
-        value = columns_ref[...]
-        for k in range(UNROLL):
-            index = step * UNROLL + k
-            value = jnp.where(lanes == index, outer_tile(index), value)
-        columns_ref[...] = value
-        return _
-
-    lax.fori_loop(0, TILES // UNROLL, outer, 0)
-    root = jnp.sqrt(1.0 + columns_ref[...].T[:TILES])
-    weight = weights[...]
-    strength = jnp.where(weight > 6.0, 0.7, jnp.where(weight > 0.0, 1.0, 0.0))
-    embed_ref[...] = -strength * root
-    rows = -0.5 * SLOPE * strength / root
-    for index in range(TILES):
-        x, y, z = tile_of(index, OWN)
-        slope[x + 1, y + 1, z + 1] = rows[index : index + 1]
-
     slope_copies = copies(slope, 1)
-    for copy in slope_copies:
-        copy.start()
-
-    def distances(index, _):
+    plane = OWN[0] * OWN[1]
+
+    def finish_density(first_z, stride_z):
+        def outer(step, _):
+            value = columns_ref[...]
+            for k in range(plane):
+                index = k * OWN[2] + first_z + stride_z * step
+                value = jnp.where(lanes == index, outer_tile(index), value)
+            columns_ref[...] = value
+            return _
+
+        lax.fori_loop(0, 2, outer, 0)
+        root = jnp.sqrt(1.0 + columns_ref[...].T[:TILES])
+        weight = weights[...]
+        strength = jnp.where(weight > 6.0, 0.7, jnp.where(weight > 0.0, 1.0, 0.0))
+        embed_ref[...] = -strength * root
+        rows = -0.5 * SLOPE * strength / root
+        for z in (first_z, first_z + stride_z):
+            for k in range(plane):
+                index = k * OWN[2] + z
+                slope[k // OWN[1] + 1, k % OWN[1] + 1, z + 1] = rows[index : index + 1]
+
+    columns_ref[...] = jnp.zeros((TILE, TILE), F32)
+    finish_density(0, OWN[2] - 1)
+    for copy, offset in zip(slope_copies, OFFSETS):
+        if offset[2] != 0:
+            copy.start()
+    finish_density(1, 1)
+    for copy, offset in zip(slope_copies, OFFSETS):
+        if offset[2] == 0:
+            copy.start()
+
+    def distances_of(index):
         x, y, z = tile_of(index, OWN)
         for k, offset in enumerate(OFFSETS):
             at = tuple(a + 1 + o for a, o in zip((x, y, z), offset))
@@ -313,9 +327,13 @@
             reach_rows[index, k : k + 1, :] = jnp.where(weight > 0.0, far, 9.0)
         for k in range(len(OFFSETS), 32):
             reach_rows[index, k : k + 1, :] = jnp.full((1, TILE), 9.0, F32)
-        return _
-
-    lax.fori_loop(0, OWN[0] * OWN[1] * OWN[2], distances, 0)
+
+    def distances(step, _):
+        for k in range(2):
+            distances_of(step * 2 + k)
+        return _
+
+    lax.fori_loop(0, TILES // 2, distances, 0)
 
     first = lax.broadcasted_iota(jnp.int32, (TILE, TILE), 0)
     second = lax.broadcasted_iota(jnp.int32, (TILE, TILE), 1)
@@ -324,7 +342,7 @@
     above_rows = ((second < first) & (second // 32 == first // 32)).astype(F32).astype(BF16)
     first_lane = (lax.broadcasted_iota(jnp.int32, (8, TILE), 1) == 0).astype(F32).astype(BF16)
 
-    def compress(group, _):
+    def compress_rows(group):
         rows = reach_rows[pl.ds(group * 4, 4)].reshape(TILE, TILE)
         near = rows < CUTOFF_SQUARED * 1.00002
         flags = near.astype(F32).astype(BF16)
@@ -349,14 +367,16 @@
             value = value.astype(F32).astype(BF16)
             value = lax.dot_general(first_lane, value, NT, preferred_element_type=F32)
             ref[:, cut] = value[0:1].astype(jnp.int32)
-        return _
-
-    lax.fori_loop(0, 4, compress, 0)
-
-    for copy in state_copies:
-        copy.wait_send()
-    for copy in slope_copies:
-        copy.wait_recv()
+
+    def compress(step, _):
+        for k in range(2):
+            compress_rows(step * 2 + k)
+        return _
+
+    lax.fori_loop(0, 2, compress, 0)
+
+    settle(wire, sends, 0)
+    settle(slope, recvs, 1)
 
     def finish(index, _):
         for z in range(EXT[2]):
@@ -368,8 +388,7 @@
         return _
 
     lax.fori_loop(0, EXT[0] * EXT[1], finish, 0)
-    for copy in slope_copies:
-        copy.wait_send()
+    settle(slope, sends, 1)
 
 
 def force_kernel(
@@ -508,8 +527,8 @@
             pltpu.VMEM(OWN + (TILE,), jnp.int32),
             pltpu.SMEM(OWN, jnp.int32),
             pltpu.SemaphoreType.DMA((3,)),
-            pltpu.SemaphoreType.DMA((2, len(OFFSETS))),
-            pltpu.SemaphoreType.DMA((2, len(OFFSETS))),
+            pltpu.SemaphoreType.DMA((2,)),
+            pltpu.SemaphoreType.DMA((2,)),
         ],
         compiler_params=pltpu.CompilerParams(collective_id=0, has_side_effects=True, vmem_limit_bytes=24 << 20),
     )(*(pltpu.with_memory_space_constraint(a, pltpu.HBM) for a in (positions, species, counts)))

time: 36.3 us -> 34.3 us (0.945)
  Pallas kernels: 35.6 us -> 33.5 us
    pallas_call x1, Pallas kernels: 27.4 us -> 25 us  [shards(): pl.pallas_call(lambda *refs: exchange_kernel(sizes, *refs), name='exchang...]
where the time goes in v5:
time: 34.3 us; the launch traced here: 34.1 us
  Pallas kernels  33.5 us (98%)
  between operations  0.64 us (2%)
    pallas_call x1, Pallas kernels, shards(): pl.pallas_call(lambda *refs: exchange_kernel(sizes, *refs), name='exchang...  25 us
    pallas_call x1, Pallas kernels, shards(): pl.pallas_call(force_kernel, name='forces', out_shape=(jax.ShapeDtypeStru...  8.48 us

profile of v5, /device:TPU:1, one launch (start us, length us, event | category | flops | bytes accessed | tf_op | source)
XLA Modules:
  0.0 34.1 jit_solution(13790067141892017210)
XLA Ops:
  0.6 25.0 %exchange.1 = (f32[4,4,6,8,128]{4,3,2,1,0:T(8,128)S(1)}, f32[16,128]{1,0:T(8,128)S(1)}, s32[16,32,128]{2,1,0:T(8,128)S(1)}, s32[1,512]{1,0:T(1,128)S(1)}, s32[1,512]{1,0:T(1,128)S(1)}) custom-call(f32[3,2,2,4,128]{4,3,2,1,0:T(4,128)} %refs_0_.1, s32[2,2,4,128]{3,2,1,0:T(4,128)} %refs_1_.1, s32[2,2,4]{2,1,0:T(2,128)} %refs_2_.1), custom_call_target="tpu_custom_call" | custom-call | tf_op jit(solution)/shard_map/exchange/pallas_call | solution.py:505
  25.6 8.5 %forces.1 = (f32[3,2,2,4,128]{4,3,2,1,0:T(4,128)}, f32[2,2,4,128]{3,2,1,0:T(4,128)}) custom-call(f32[4,4,6,8,128]{4,3,2,1,0:T(8,128)S(1)} %get-tuple-element.7.full_ref, f32[16,128]{1,0:T(8,128)S(1)} %get-tuple-element.8.embed_ref, s32[16,32,128]{2,1,0:T(8,128)S(1)} %get-tuple-element.9.near_ref, s32[1,512]{1,0:T(1,128)S(1)} %get-tuple-element.10.begin_ref, ...), custom_call_target="tpu_custom_call" | custom-call | tf_op jit(solution)/shard_map/forces/pallas_call | solution.py:535

commit v6 on v5

--- a/solution.py
+++ b/solution.py
@@ -24,7 +24,7 @@
 SLOPE = ALPHA / (5.0 * BETA)
 PART = 128
 TILES = OWN[0] * OWN[1] * OWN[2]
-UNROLL = 4
+UNROLL = OWN[2]
 FORCE_PART = 64
 GROUP = 6
 HIGHEST = lax.Precision.HIGHEST
@@ -200,12 +200,14 @@
         ) + value[:, :TILE]
 
     def window(column, z, width=3):
+        if isinstance(z, int):
+            return beside[column, :, z * TILE : (z + width) * TILE]
         return beside[column, :, pl.ds(pl.multiple_of(z * TILE, TILE), width * TILE)]
 
     parts = TILE // PART
 
-    def inner_tile(index):
-        x, y, z = tile_of(index, OWN)
+    def inner_tile(step, z):
+        x, y, index = step // OWN[1], lax.rem(step, OWN[1]), step * OWN[2] + z
         for part in range(parts):
             cut = slice(part * PART, (part + 1) * PART)
             rows = own[index, cut]
@@ -225,7 +227,7 @@
 
     def inner(step, _):
         for k in range(UNROLL):
-            inner_tile(step * UNROLL + k)
+            inner_tile(step, k)
         return _
 
     lax.fori_loop(0, TILES // UNROLL, inner, 0)
@@ -313,27 +315,28 @@
         if offset[2] == 0:
             copy.start()
 
-    def distances_of(index):
-        x, y, z = tile_of(index, OWN)
+    def distances_of(step, z):
+        x, y, index = step // OWN[1], lax.rem(step, OWN[1]), step * OWN[2] + z
+        around, known = (ref.at[pl.ds(x, 3), pl.ds(y, 3)] for ref in (wire, full_ref))
         for k, offset in enumerate(OFFSETS):
-            at = tuple(a + 1 + o for a, o in zip((x, y, z), offset))
-            there = wire[at]
+            at = (offset[0] + 1, offset[1] + 1, z + 1 + offset[2])
+            there = around[at]
             far = None
             for comp, o in enumerate(offset):
                 if o:
                     gap = there[comp : comp + 1] if o > 0 else 1.0 - there[comp : comp + 1]
                     far = gap * gap if far is None else far + gap * gap
-            weight = full_ref[at + (slice(3, 4),)]
+            weight = known[at + (slice(3, 4),)]
             reach_rows[index, k : k + 1, :] = jnp.where(weight > 0.0, far, 9.0)
         for k in range(len(OFFSETS), 32):
             reach_rows[index, k : k + 1, :] = jnp.full((1, TILE), 9.0, F32)
 
     def distances(step, _):
-        for k in range(2):
-            distances_of(step * 2 + k)
-        return _
-
-    lax.fori_loop(0, TILES // 2, distances, 0)
+        for k in range(UNROLL):
+            distances_of(step, k)
+        return _
+
+    lax.fori_loop(0, TILES // UNROLL, distances, 0)
 
     first = lax.broadcasted_iota(jnp.int32, (TILE, TILE), 0)
     second = lax.broadcasted_iota(jnp.int32, (TILE, TILE), 1)
@@ -354,9 +357,9 @@
             moved = pltpu.roll(word, TILE - (1 << bit), 1)
             stay = jnp.where((word & (1 << bit)) != 0, 0, word)
             word = jnp.where((moved & (1 << bit)) != 0, moved, stay)
-        for bit in range(7):
-            word = jnp.where((filled & (1 << bit)) != 0, pltpu.roll(word, 1 << bit, 1), word)
         start = filled & (TILE - 1)
+        turned = (second - start) & (TILE - 1)
+        word = jnp.take_along_axis(word, turned, axis=1, mode="promise_in_bounds")
         code = ((word >> 7) & 127) + jnp.where(second < start, TILE, 0)
         near_ref[pl.ds(group * 4, 4)] = jnp.where(word >= 16384, code, 512).reshape(4, 32, TILE)
         cut = pl.ds(pl.multiple_of(group * TILE, TILE), TILE)
@@ -396,29 +399,31 @@
 ):
     row = lax.broadcasted_iota(jnp.int32, (8, TILE), 0)
 
-    def pack_tile(index):
-        x, y, z = tile_of(index, OWN)
-        packed[index, 0] = full_ref[x + 1, y + 1, z + 1]
+    def pack_tile(step, z):
+        x, y, index = step // OWN[1], lax.rem(step, OWN[1]), step * OWN[2] + z
+        around = full_ref.at[pl.ds(x, 3), pl.ds(y, 3)]
+        chosen = packed.at[index]
+        chosen[0] = around[1, 1, z + 1]
         current = jnp.zeros((8, TILE), F32)
         chunk = begin_ref[0, index * 32]
         for k, offset in enumerate(OFFSETS):
-            there = full_ref[tuple(a + 1 + o for a, o in zip((x, y, z), offset))]
+            there = around[offset[0] + 1, offset[1] + 1, z + 1 + offset[2]]
             code = jnp.broadcast_to(near_ref[index, k : k + 1, :], (8, TILE))
             places = code & (TILE - 1)
             value = jnp.take_along_axis(there, places, axis=1, mode="promise_in_bounds")
             merged = jnp.where(code < TILE, value, current)
             beyond = jnp.where((code & TILE) != 0, value, 0.0)
-            packed[index, chunk] = merged
-            packed[index, chunk + 1] = beyond
+            chosen[chunk] = merged
+            chosen[chunk + 1] = beyond
             later = begin_ref[0, index * 32 + k + 1]
             current = jnp.where(later > chunk, beyond, merged)
             chunk = later
         for k in range(1, GROUP + 1):
-            packed[index, chunk + k] = jnp.zeros((8, TILE), F32)
+            chosen[chunk + k] = jnp.zeros((8, TILE), F32)
 
     def pack(step, _):
         for k in range(UNROLL):
-            pack_tile(step * UNROLL + k)
+            pack_tile(step, k)
         return _
 
     lax.fori_loop(0, TILES // UNROLL, pack, 0)

time: 34.3 us -> 33.9 us (0.988)
  Pallas kernels: 33.5 us -> 33.1 us
    pallas_call x1, Pallas kernels: 8.48 us -> 8.11 us  [shards(): pl.pallas_call(force_kernel, name='forces', out_shape=(jax.ShapeDtypeStru...]
where the time goes in v6:
time: 33.9 us; the launch traced here: 33.8 us
  Pallas kernels  33.1 us (98%)
  between operations  0.64 us (2%)
    pallas_call x1, Pallas kernels, shards(): pl.pallas_call(lambda *refs: exchange_kernel(sizes, *refs), name='exchang...  25 us
    pallas_call x1, Pallas kernels, shards(): pl.pallas_call(force_kernel, name='forces', out_shape=(jax.ShapeDtypeStru...  8.11 us

profile of v6, /device:TPU:1, one launch (start us, length us, event | category | flops | bytes accessed | tf_op | source)
XLA Modules:
  0.0 33.8 jit_solution(9747884317730185956)
XLA Ops:
  0.6 25.0 %exchange.1 = (f32[4,4,6,8,128]{4,3,2,1,0:T(8,128)S(1)}, f32[16,128]{1,0:T(8,128)S(1)}, s32[16,32,128]{2,1,0:T(8,128)S(1)}, s32[1,512]{1,0:T(1,128)S(1)}, s32[1,512]{1,0:T(1,128)S(1)}) custom-call(f32[3,2,2,4,128]{4,3,2,1,0:T(4,128)} %refs_0_.1, s32[2,2,4,128]{3,2,1,0:T(4,128)} %refs_1_.1, s32[2,2,4]{2,1,0:T(2,128)} %refs_2_.1), custom_call_target="tpu_custom_call" | custom-call | tf_op jit(solution)/shard_map/exchange/pallas_call | solution.py:510
  25.6 8.1 %forces.1 = (f32[3,2,2,4,128]{4,3,2,1,0:T(4,128)}, f32[2,2,4,128]{3,2,1,0:T(4,128)}) custom-call(f32[4,4,6,8,128]{4,3,2,1,0:T(8,128)S(1)} %get-tuple-element.7.full_ref, f32[16,128]{1,0:T(8,128)S(1)} %get-tuple-element.8.embed_ref, s32[16,32,128]{2,1,0:T(8,128)S(1)} %get-tuple-element.9.near_ref, s32[1,512]{1,0:T(1,128)S(1)} %get-tuple-element.10.begin_ref, ...), custom_call_target="tpu_custom_call" | custom-call | tf_op jit(solution)/shard_map/forces/pallas_call | solution.py:540

commit v7 on v6

--- a/solution.py
+++ b/solution.py
@@ -135,24 +135,26 @@
                 weights[index : index + 1, :] = weight
     pl.semaphore_wait(barrier, len(OFFSETS))
 
-    def copies(ref, which):
+    def copies(ref, which, arrival):
         return [
             pltpu.make_async_remote_copy(
                 src_ref=ref.at[region(offset, True)],
                 dst_ref=ref.at[region(offset, False)],
                 send_sem=sends.at[which],
-                recv_sem=recvs.at[which],
+                recv_sem=recvs.at[arrival(offset)],
                 device_id=peer(offset),
                 device_id_type=MESH,
             )
             for offset in OFFSETS
         ]
 
-    def settle(ref, sems, which):
-        whole = ref.at[:, :, 0 : EXT[2] - 1]
-        pltpu.make_async_copy(whole, whole, sems.at[which]).wait()
-
-    state_copies = copies(wire, 0)
+    def settle(part, sem):
+        pltpu.make_async_copy(part, part, sem).wait()
+
+    sides = wire.at[0:2, :, 0:4]
+    others = wire.at[:, 0:3, 0:4]
+
+    state_copies = copies(wire, 0, lambda o: 0 if o[2] == 0 and 0 in o[:2] else 1)
     for copy in state_copies:
         copy.start()
 
@@ -180,7 +182,8 @@
     def prepare_own(index, _):
         x, y = 1 + index // OWN[1], 1 + index % OWN[1]
         for z in (0, EXT[2] - 1):
-            beside[x * EXT[1] + y, :, z * TILE : (z + 1) * TILE] = jnp.zeros((48, TILE), BF16)
+            for column in range(4):
+                beside[index * 4 + column, :, z * TILE : (z + 1) * TILE] = jnp.zeros((48, TILE), BF16)
         for z in range(OWN[2]):
             full = prepare(x, y, z + 1)
             row = lax.broadcasted_iota(jnp.int32, (8, TILE), 0)
@@ -232,85 +235,101 @@
 
     lax.fori_loop(0, TILES // UNROLL, inner, 0)
 
-    settle(wire, recvs, 0)
-
-    def prepare_side(index, _):
-        x = jnp.where(index < 4, 0, jnp.where(index < 8, EXT[0] - 1, 1 + (index - 8) // 2))
-        y = jnp.where(index < 8, lax.rem(index, 4), (EXT[1] - 1) * lax.rem(index, 2))
+    settle(sides, recvs.at[0])
+    last_x, last_y = EXT[0] - 1, EXT[1] - 1
+
+    def side_column(index):
+        half, which = index % 4 // 2, index % 2
+        x = jnp.where(index < 4, half * last_x, 1 + half)
+        y = jnp.where(index < 4, 1 + which, which * last_y)
+        return x, y
+
+    def prepare_sides(index, _):
+        x, y = side_column(index)
+        for z in range(1, EXT[2] - 1):
+            prepare(x, y, z)
+        return _
+
+    lax.fori_loop(0, 8, prepare_sides, 0)
+
+    def columns_beside(x, y):
+        side_x, side_y = x * last_x, y * last_y
+        beside_x = [side_x * EXT[1] + 1 + dy for dy in range(OWN[1])]
+        beside_y = [(1 + dx) * EXT[1] + side_y for dx in range(OWN[0])]
+        return beside_x + beside_y, side_x * EXT[1] + side_y
+
+    def middle(step, _):
+        x, y = step // OWN[1], lax.rem(step, OWN[1])
+        for z in range(OWN[2]):
+            index = step * OWN[2] + z
+            total = totals[index]
+            for column in columns_beside(x, y)[0]:
+                total = total + blocks(cubes(own[index], window(column, z)))
+            totals[index] = total
+        return _
+
+    lax.fori_loop(0, OWN[0] * OWN[1], middle, 0)
+
+    settle(others, recvs.at[1])
+
+    def prepare_corners(index, _):
         for z in range(EXT[2]):
+            prepare((index // 2) * last_x, lax.rem(index, 2) * last_y, z)
+        return _
+
+    lax.fori_loop(0, 4, prepare_corners, 0)
+
+    def prepare_ends(index, _):
+        side = side_column(jnp.maximum(index - 4, 0))
+        x = jnp.where(index < 4, 1 + index // 2, side[0])
+        y = jnp.where(index < 4, 1 + lax.rem(index, 2), side[1])
+        for z in (0, EXT[2] - 1):
             prepare(x, y, z)
         return _
 
-    lax.fori_loop(0, EXT[0] * EXT[1] - OWN[0] * OWN[1], prepare_side, 0)
-
-    def prepare_ends(index, _):
-        for z in (0, EXT[2] - 1):
-            prepare(1 + index // OWN[1], 1 + index % OWN[1], z)
-        return _
-
-    lax.fori_loop(0, OWN[0] * OWN[1], prepare_ends, 0)
-
-    def ends_tile(index):
-        column, upper = index // 2, lax.rem(index, 2)
-        tile = column * OWN[2] + upper * (OWN[2] - 1)
-        for part in range(parts):
-            cut = slice(part * PART, (part + 1) * PART)
-            rows = own[tile, cut]
-            total = totals[tile, cut]
-            for x in range(OWN[0]):
-                for y in range(OWN[1]):
-                    there = (x + 1) * EXT[1] + y + 1
-                    total = total + cubes(rows, window(there, upper * (EXT[2] - 1), 1))
-            totals[tile, cut] = total
-
-    def ends(step, _):
-        for k in range(UNROLL):
-            ends_tile(step * UNROLL + k)
-        return _
-
-    lax.fori_loop(0, 2 * OWN[0] * OWN[1] // UNROLL, ends, 0)
-
+    lax.fori_loop(0, 12, prepare_ends, 0)
     lanes = lax.broadcasted_iota(jnp.int32, (TILE, TILE), 1)
 
-    def outer_tile(index):
-        x, y, z = tile_of(index, OWN)
-        side_x, side_y = x * (EXT[0] - 1), y * (EXT[1] - 1)
-        columns = [side_x * EXT[1] + y + dy for dy in range(3)]
-        columns += [(dx + 1) * EXT[1] + side_y for dx in range(OWN[0])]
-        total = totals[index]
-        for column in columns:
-            total = total + blocks(cubes(own[index], window(column, z)))
+    def outer_tile(step, z):
+        x, y, index = step // OWN[1], lax.rem(step, OWN[1]), step * OWN[2] + z
+        near, corner = columns_beside(x, y)
+        total = totals[index] + blocks(cubes(own[index], window(corner, z)))
+        if z in (0, OWN[2] - 1):
+            near = near + [(1 + dx) * EXT[1] + 1 + dy for dx in range(2) for dy in range(2)]
+            there = [window(column, 0 if z == 0 else EXT[2] - 1, 1) for column in near]
+            for k in range(0, 8, 2):
+                pair = jnp.concatenate(there[k : k + 2], axis=1)
+                total = total + blocks(cubes(own[index], pair))
         return jnp.sum(total, axis=1, keepdims=True)
 
-    slope_copies = copies(slope, 1)
+    slope_copies = copies(slope, 1, lambda o: 2)
     plane = OWN[0] * OWN[1]
 
-    def finish_density(first_z, stride_z):
+    def finish_density(heights):
         def outer(step, _):
             value = columns_ref[...]
-            for k in range(plane):
-                index = k * OWN[2] + first_z + stride_z * step
-                value = jnp.where(lanes == index, outer_tile(index), value)
+            for z in heights:
+                value = jnp.where(lanes == step * OWN[2] + z, outer_tile(step, z), value)
             columns_ref[...] = value
             return _
 
-        lax.fori_loop(0, 2, outer, 0)
+        lax.fori_loop(0, plane, outer, 0)
         root = jnp.sqrt(1.0 + columns_ref[...].T[:TILES])
         weight = weights[...]
         strength = jnp.where(weight > 6.0, 0.7, jnp.where(weight > 0.0, 1.0, 0.0))
         embed_ref[...] = -strength * root
         rows = -0.5 * SLOPE * strength / root
-        for z in (first_z, first_z + stride_z):
+        for z in heights:
             for k in range(plane):
                 index = k * OWN[2] + z
                 slope[k // OWN[1] + 1, k % OWN[1] + 1, z + 1] = rows[index : index + 1]
 
     columns_ref[...] = jnp.zeros((TILE, TILE), F32)
-    finish_density(0, OWN[2] - 1)
+    finish_density((0, OWN[2] - 1))
     for copy, offset in zip(slope_copies, OFFSETS):
         if offset[2] != 0:
             copy.start()
-    finish_density(1, 1)
+    finish_density((1, 2))
     for copy, offset in zip(slope_copies, OFFSETS):
         if offset[2] == 0:
             copy.start()
@@ -378,8 +397,8 @@
 
     lax.fori_loop(0, 2, compress, 0)
 
-    settle(wire, sends, 0)
-    settle(slope, recvs, 1)
+    settle(wire.at[:, :, 0 : EXT[2] - 1], sends.at[0])
+    settle(slope.at[:, :, 0 : EXT[2] - 1], recvs.at[2])
 
     def finish(index, _):
         for z in range(EXT[2]):
@@ -391,7 +410,7 @@
         return _
 
     lax.fori_loop(0, EXT[0] * EXT[1], finish, 0)
-    settle(slope, sends, 1)
+    settle(slope.at[:, :, 0 : EXT[2] - 1], sends.at[1])
 
 
 def force_kernel(
@@ -533,7 +552,7 @@
             pltpu.SMEM(OWN, jnp.int32),
             pltpu.SemaphoreType.DMA((3,)),
             pltpu.SemaphoreType.DMA((2,)),
-            pltpu.SemaphoreType.DMA((2,)),
+            pltpu.SemaphoreType.DMA((3,)),
         ],
         compiler_params=pltpu.CompilerParams(collective_id=0, has_side_effects=True, vmem_limit_bytes=24 << 20),
     )(*(pltpu.with_memory_space_constraint(a, pltpu.HBM) for a in (positions, species, counts)))

time: 33.9 us -> 35.4 us (1.044)
  Pallas kernels: 33.1 us -> 34.6 us
    pallas_call x1, Pallas kernels: 25 us -> 26.5 us  [shards(): pl.pallas_call(lambda *refs: exchange_kernel(sizes, *refs), name='exchang...]
where the time goes in v7:
time: 35.4 us; the launch traced here: 35.2 us
  Pallas kernels  34.6 us (98%)
  between operations  0.64 us (2%)
    pallas_call x1, Pallas kernels, shards(): pl.pallas_call(lambda *refs: exchange_kernel(sizes, *refs), name='exchang...  26.5 us
    pallas_call x1, Pallas kernels, shards(): pl.pallas_call(force_kernel, name='forces', out_shape=(jax.ShapeDtypeStru...  8.11 us

profile of v7, /device:TPU:1, one launch (start us, length us, event | category | flops | bytes accessed | tf_op | source)
XLA Modules:
  0.0 35.2 jit_solution(14706307288653595641)
XLA Ops:
  0.6 26.5 %exchange.1 = (f32[4,4,6,8,128]{4,3,2,1,0:T(8,128)S(1)}, f32[16,128]{1,0:T(8,128)S(1)}, s32[16,32,128]{2,1,0:T(8,128)S(1)}, s32[1,512]{1,0:T(1,128)S(1)}, s32[1,512]{1,0:T(1,128)S(1)}) custom-call(f32[3,2,2,4,128]{4,3,2,1,0:T(4,128)} %refs_0_.1, s32[2,2,4,128]{3,2,1,0:T(4,128)} %refs_1_.1, s32[2,2,4]{2,1,0:T(2,128)} %refs_2_.1), custom_call_target="tpu_custom_call" | custom-call | tf_op jit(solution)/shard_map/exchange/pallas_call | solution.py:529
  27.1 8.1 %forces.1 = (f32[3,2,2,4,128]{4,3,2,1,0:T(4,128)}, f32[2,2,4,128]{3,2,1,0:T(4,128)}) custom-call(f32[4,4,6,8,128]{4,3,2,1,0:T(8,128)S(1)} %get-tuple-element.7.full_ref, f32[16,128]{1,0:T(8,128)S(1)} %get-tuple-element.8.embed_ref, s32[16,32,128]{2,1,0:T(8,128)S(1)} %get-tuple-element.9.near_ref, s32[1,512]{1,0:T(1,128)S(1)} %get-tuple-element.10.begin_ref, ...), custom_call_target="tpu_custom_call" | custom-call | tf_op jit(solution)/shard_map/forces/pallas_call | solution.py:559
